TPU v7x, 128 devices: a whole 4x4x4 slice. The times are simulated.
128 devices in a mesh: hist: 8 (over z_hi, x), tcol: 16 (over z_lo, y, core).
Axes of the slice: x: 4, y: 4, z: 4 (z_hi: 2, z_lo: 2; z = z_hi * 2 + z_lo), core: 2. Of those that a mesh axis runs over, the one named last changes fastest.
Arguments:
- history: float32 [16384, 8192], P('hist', 'tcol'), may hold values from -5 to 5
- memory_weight_first: float32 [512, 16384], P(None, 'hist'), may hold values from -0.0625 to 0.0625
- memory_weight_second: float32 [512, 16384], P(None, 'hist'), may hold values from -0.0625 to 0.0625
- link: float32 [512, 512], replicated, may hold values from -0.25 to 0.25
- propagator: float32 [8192, 8192], P(None, 'tcol'), may hold values from -0.0625 to 0.0625
- inverse_one: float32 [512, 512], replicated, as said below
- inverse_two: float32 [512, 512], replicated, as said below
- explicit_first: float32 [512, 8192], P(None, 'tcol'), may hold values from -5 to 5
- explicit_second: float32 [512, 8192], P(None, 'tcol'), may hold values from -5 to 5
Outputs:
- first_slab_rows: float32 [512, 8192], P('hist', 'tcol')
- slab_two: float32 [512, 8192], P('hist', 'tcol')
Inputs may be any that keep to these rules, and one draw needn't show every extreme that they name: `inverse_one`: the identity plus independent entries of deviation 0.5 / sqrt(512). `inverse_two`: the identity plus independent entries of deviation 0.5 / sqrt(512).
All inputs are finite; a program needn't handle non-finite values.
Results may differ from a plain program's by a relative error of at most 0.0003.
Values sent between devices are 32-bit elements; how exact they have to be, the bound alone decides.
No kernel may reach another device: no remote copies, remote signals or barrier semaphores. Data moves between devices by JAX's collectives and lax.ppermute only.
A program may use at most 128 MiB of HBM per device.

v0:
```python
import jax
import jax.numpy as jnp
from jax import lax
from jax.experimental import pallas as pl
from jax.experimental.pallas import tpu as pltpu
from jax.sharding import PartitionSpec as P


strength = 0.2
step_size = 0.5
F32, BF16 = jnp.float32, jnp.bfloat16
WHOLE = pl.BlockSpec(memory_space=pltpu.VMEM)
SCALARS = pl.BlockSpec(memory_space=pltpu.SMEM)
CHUNKS = (256, 256, 512, 512, 512)
LANES = 128
UNREAD = pl.BlockSpec(memory_space=pl.ANY)

CHIPS = ((0, 0), (0, 1), (1, 1), (1, -1), (0, -1), (1, 0), (0, 2), (1, 2))


def move_hist(value, dz, dx):
    pairs = [(i, ((i >> 2) ^ dz) * 4 + ((i & 3) + dx) % 4) for i in range(8)]
    return lax.ppermute(value, "hist", pairs)


def move_tcol(value, dz, dy):
    def target(i):
        y = ((i >> 1) + (-dy if i & 1 else dy)) % 4
        return ((i >> 3) ^ dz) * 8 + y * 2 + (i & 1)

    return lax.ppermute(value, "tcol", [(i, target(i)) for i in range(16)])


def other_core(value):
    return lax.ppermute(value, "tcol", [(i, i ^ 1) for i in range(16)])


def cubic_power(value):
    return strength * value * value * value


def split(value):
    high = value.astype(BF16)
    return high, (value - high.astype(F32)).astype(BF16)


def product(left, right):
    def dot(a, b):
        return jnp.dot(a, b, preferred_element_type=F32)

    return dot(left[0], right[0]) + (dot(left[0], right[1]) + dot(left[1], right[0]))


def narrow_product(left, right):
    n = right[0].shape[1]
    wide = jnp.dot(left[0], jnp.concatenate(right, axis=1), preferred_element_type=F32)
    low = jnp.dot(left[1], right[0], preferred_element_type=F32)
    return wide[:, :n] + (wide[:, n:] + low)


def total(refs):
    value = refs[0][...]
    for ref in refs[1:]:
        value = value + ref[...]
    return value


def rows_from(start, count):
    return pl.ds(pl.multiple_of(start, count), count)


def call(kernel, outs, where, inputs, after=(), scratch=()):
    n = len(after)

    def body(at, *refs):
        kernel(at, *refs[: len(inputs)], *refs[len(inputs) + n :])

    return pl.pallas_call(
        body,
        in_specs=[SCALARS] + [WHOLE] * len(inputs) + [UNREAD] * n,
        out_shape=[jax.ShapeDtypeStruct(shape, dtype) for shape, dtype in outs],
        out_specs=[WHOLE] * len(outs),
        scratch_shapes=[pltpu.VMEM(shape, F32) for shape in scratch],
        compiler_params=pltpu.CompilerParams(vmem_limit_bytes=8 << 20),
    )(where, *inputs, *after)


def in_hbm(array):
    return pltpu.with_memory_space_constraint(array, pltpu.HBM)


def lanes_from(block):
    return pl.ds(pl.multiple_of(block * LANES, LANES), LANES)


def collect(history, weights, where, cut, after=()):
    depth, cols = history.shape
    rows = weights.shape[0]
    half = rows // 2
    n = len(after)
    ends = [depth * sum(CHUNKS[: r + 1]) // sum(CHUNKS) for r in range(len(CHUNKS))]
    steps = len(ends)
    shapes = [(2, half, LANES)] * 4 if cut else [(rows, cols)]

    def kernel(at, hist_ref, weight_ref, *rest):
        outs = rest[n : n + len(shapes)]
        hist, weight, arrived = rest[n + len(shapes) : n + len(shapes) + 3]
        acc = rest[-1] if cut else outs[0]
        copies = []
        for r in range(steps):
            lines = slice(ends[r - 1] if r else 0, ends[r])
            pair = (
                pltpu.make_async_copy(hist_ref.at[lines, :], hist.at[lines, :], arrived.at[r, 0]),
                pltpu.make_async_copy(
                    weight_ref.at[:, lines], weight.at[:, lines], arrived.at[r, 1]
                ),
            )
            for copy in pair:
                copy.start()
            copies.append((lines, pair))
        for r, (lines, pair) in enumerate(copies):
            for copy in pair:
                copy.wait()
            value = product(split(weight[:, lines]), split(cubic_power(hist[lines, :])))
            acc[...] = value if r == 0 else acc[...] + value
        if cut:
            for near in range(2):
                lines = rows_from((at[0] ^ (1 - near)) * half, half)
                for d in range(4):
                    outs[d][near] = acc[lines, lanes_from((at[1] + d) & 3)]

    scratch = [
        pltpu.VMEM((depth, cols), F32),
        pltpu.VMEM((rows, depth), F32),
        pltpu.SemaphoreType.DMA((steps, 2)),
    ]
    return pl.pallas_call(
        kernel,
        in_specs=[SCALARS, UNREAD, UNREAD] + [UNREAD] * n,
        out_specs=[WHOLE] * len(shapes),
        scratch_shapes=scratch + ([pltpu.VMEM((rows, cols), F32)] if cut else []),
        out_shape=[jax.ShapeDtypeStruct(shape, F32) for shape in shapes],
        name="collect",
        compiler_params=pltpu.CompilerParams(vmem_limit_bytes=20 << 20),
    )(where, in_hbm(history), in_hbm(weights), *after)


def cut_sums(sums, where, after):
    def kernel(at, sums_ref, *outs):
        for d in range(4):
            outs[d][...] = sums_ref[:, lanes_from((at[1] + d) & 3)]

    outs = [((sums.shape[0], LANES), F32)] * 4
    return call(kernel, outs, where, [sums], after)


def split_propagator(propagator, where, after):
    cols = propagator.shape[1]
    blocks = in_hbm(propagator.reshape(16, 4, LANES, cols))

    def kernel(at, blocks_ref, _, *refs):
        outs, held, arrived = refs[:4], refs[4], refs[5]
        copies = [
            pltpu.make_async_copy(blocks_ref.at[at[k], at[16]], held.at[k], arrived.at[k])
            for k in range(16)
        ]
        for copy in copies:
            copy.start()
        for k, copy in enumerate(copies):
            copy.wait()
            lines = slice((k & 7) * LANES, ((k & 7) + 1) * LANES)
            high, low = split(held[k])
            outs[2 * (k >> 3)][lines, :], outs[2 * (k >> 3) + 1][lines, :] = high, low

    return pl.pallas_call(
        kernel,
        in_specs=[SCALARS, UNREAD, UNREAD],
        out_specs=[WHOLE] * 4,
        scratch_shapes=[pltpu.VMEM((16, LANES, cols), F32), pltpu.SemaphoreType.DMA((16,))],
        out_shape=[jax.ShapeDtypeStruct((8 * LANES, cols), BF16)] * 4,
        name="split_propagator",
        compiler_params=pltpu.CompilerParams(vmem_limit_bytes=12 << 20),
    )(where, blocks, after)


def own_explicit(explicit_one, explicit_two, where, after):
    size = explicit_one.shape[0]

    def kernel(at, first_ref, second_ref, _, first_out, second_out):
        first_out[...] = first_ref[...]
        second_out[...] = second_ref[...]

    return pl.pallas_call(
        kernel,
        grid_spec=pltpu.PrefetchScalarGridSpec(
            num_scalar_prefetch=1,
            grid=(1,),
            in_specs=[
                pl.BlockSpec((size // 2, LANES), lambda i, at: (at[0], at[1])),
                pl.BlockSpec((size, LANES), lambda i, at: (0, at[1])),
                UNREAD,
            ],
            out_specs=[WHOLE] * 2,
        ),
        out_shape=[
            jax.ShapeDtypeStruct((size // 2, LANES), F32),
            jax.ShapeDtypeStruct((size, LANES), F32),
        ],
        name="own_explicit",
        compiler_params=pltpu.CompilerParams(vmem_limit_bytes=4 << 20),
    )(where, in_hbm(explicit_one), in_hbm(explicit_two), after)


def split_matrices(matrices, where, after):
    size = matrices[0].shape[0]
    half = size // 2

    def kernel(at, *refs):
        for n in range(2):
            refs[3 + 2 * n][...], refs[4 + 2 * n][...] = split(refs[n][...])
        refs[7][...], refs[8][...] = split(refs[2][rows_from(at[0] * half, half), :])

    outs = [((size, size), BF16)] * 4 + [((half, size), BF16)] * 2
    return call(kernel, outs, where, matrices, after)


def predict(explicit, parts, where, after):
    def kernel(at, *refs):
        pred = total(refs[:-2])
        refs[-2][...] = pred
        refs[-1][...] = cubic_power(pred)

    outs = [(explicit.shape, F32)] * 2
    return call(kernel, outs, where, [explicit, *parts], after)


def side_by_side(refs):
    return jnp.concatenate([ref[...] for ref in refs], axis=1)


def times(split_rows, blocks, span):
    return product(split(blocks), (split_rows[0][span, :], split_rows[1][span, :]))


def propagate(split_rows, blocks, where, span, begun=(), stacked=False):
    n = len(blocks)

    def kernel(at, high_ref, low_ref, *refs):
        joined = side_by_side(refs[:n])
        value = times((high_ref, low_ref), joined, span)
        for ref in refs[n : n + len(begun)]:
            value = value + ref[...]
        refs[n + len(begun)][...] = value
        if stacked:
            refs[-1][...] = joined

    rows = blocks[0].shape[0]
    outs = [((rows, split_rows[0].shape[1]), F32)]
    if stacked:
        outs.append(((rows, span.stop - span.start), F32))
    return call(kernel, outs, where, [*split_rows, *blocks, *begun])


def finish_first(split_rows, blocks, where, span, begun):
    n = len(blocks)

    def kernel(at, high_ref, low_ref, *refs):
        acc = refs[-1]
        acc[...] = refs[n][...] + times((high_ref, low_ref), side_by_side(refs[:n]), span)
        for d in range(4):
            refs[n + 1 + d][...] = acc[:, lanes_from((at[1] + d) & 3)]

    rows, cols = begun.shape
    outs = [((rows, LANES), F32)] * 4
    inputs = [*split_rows, *blocks, begun]
    return call(kernel, outs, where, inputs, (), [(rows, cols)])


def finish_second(split_rows, blocks, where, span, begun, kept):
    n = len(blocks)
    rows, cols = begun.shape
    part = rows // 4

    def kernel(at, high_ref, low_ref, *refs):
        outs, acc = refs[n + 2 : -1], refs[-1]
        acc[...] = refs[n][...] + times((high_ref, low_ref), side_by_side(refs[:n]), span)
        mine = lanes_from(at[1])
        acc[:, mine] = acc[:, mine] + refs[n + 1][...]
        for d in range(4):
            outs[d][...] = acc[rows_from(((at[1] + d) & 3) * part, part), :]

    outs = [((part, cols), F32)] * 4
    inputs = [*split_rows, *blocks, begun, kept]
    return call(kernel, outs, where, inputs, (), [(rows, cols)])


def right_side(pred, parts, where):
    def kernel(at, pred_ref, *refs):
        refs[-1][...] = pred_ref[...] + step_size * total(refs[:-1])

    return call(kernel, [(pred.shape, F32)], where, [pred, *parts])[0]


def solve(right_own, right_other, matrices, explicit_two, near_own, near_other, where):
    half = right_own.shape[0]
    part = half // 4

    def kernel(at, own_ref, other_ref, explicit_ref, near_ref, far_ref, *rest):
        mats, (moved_ref, kept_ref), pieces = rest[:6], rest[6:8], rest[8:12]
        right, first = rest[12:]
        right[rows_from(at[0] * half, half), :] = own_ref[...]
        right[rows_from((at[0] ^ 1) * half, half), :] = other_ref[...]
        first[...] = narrow_product((mats[0][...], mats[1][...]), split(right[...]))
        pred = explicit_ref[...] + (near_ref[...] + far_ref[...])
        pred = pred + narrow_product((mats[2][...], mats[3][...]), split(cubic_power(first[...])))
        both = jnp.concatenate([step_size * cubic_power(pred), pred], axis=1)
        solved = product((mats[4][...], mats[5][...]), split(both))
        moved_ref[...] = solved[:, :LANES]
        kept_ref[...] = solved[:, LANES:]
        for d in range(4):
            pieces[d][...] = first[rows_from((at[0] * 4 + ((at[1] + d) & 3)) * part, part), :]

    outs = [((half, LANES), F32)] * 2 + [((part, LANES), F32)] * 4
    inputs = [right_own, right_other, explicit_two, near_own, near_other, *matrices]
    return call(kernel, outs, where, inputs, (), [(2 * half, LANES)] * 2)


def add_pairs(blocks, where, after):
    def kernel(at, *refs):
        ins, far_ref, keep_ref = refs[:4], refs[4], refs[5]
        far_ref[...] = (ins[0][0] + ins[1][0]) + (ins[2][0] + ins[3][0])
        keep_ref[...] = (ins[0][1] + ins[1][1]) + (ins[2][1] + ins[3][1])

    return call(kernel, [(blocks[0].shape[1:], F32)] * 2, where, blocks, after)


def add_blocks(blocks, where, after):
    def kernel(at, *refs):
        refs[-1][...] = total(refs[:-1])

    return call(kernel, [(blocks[0].shape, F32)], where, blocks, after)[0]


def last_rows(pieces, parts, where):
    part, cols = parts[0].shape

    def kernel(at, *refs):
        first_ref, second_ref = refs[8], refs[9]
        second_ref[...] = total(refs[4:8])
        for ref, d in zip(refs[:4], (0, 2, 1, 3)):
            first_ref[:, lanes_from((at[1] - d) & 3)] = ref[...]

    outs = [((part, cols), F32)] * 2
    return call(kernel, outs, where, [*pieces, *parts])


def shards(
    history,
    memory_weight_first,
    memory_weight_second,
    link,
    propagator,
    inverse_one,
    inverse_two,
    explicit_first,
    explicit_second,
):
    h = lax.axis_index("hist")
    t = lax.axis_index("tcol")
    z, x = h >> 2, h & 3
    chip_z, chip_y, core = t >> 3, (t >> 1) & 3, t & 1

    def numbers(*values):
        return jnp.stack([v.astype(jnp.int32) for v in values])

    zx = numbers(z, x)
    sources = [
        (chip_z ^ dz) * 8 + ((chip_y - dy * (1 - 2 * c)) & 3) * 2 + c
        for c in (core, 1 - core)
        for dz, dy in CHIPS
    ]
    early = 6
    span_early, span_late = slice(0, early * LANES), slice(early * LANES, 8 * LANES)

    def over_x(blocks):
        return [blocks[0]] + [move_hist(blocks[d], 0, d) for d in (2, 1, 3)]

    def gathered(value):
        mine, theirs = rows[:2], rows[2:]
        own = [value] + [move_tcol(value, dz, dy) for dz, dy in CHIPS[1:6]]
        own += [move_tcol(own[1], 0, 1), move_tcol(own[2], 0, 1)]
        begun, stack = propagate(mine, own[:early], zx, span_early, (), True)
        first = other_core(stack)
        begun, stack = propagate(mine, own[early:], zx, span_late, [begun], True)
        last = other_core(stack)
        return propagate(theirs, [first], zx, span_early, [begun])[0], last

    blocks = collect(history, memory_weight_first, zx, True)
    pairs = over_x(blocks)
    sums = collect(history, memory_weight_second, zx, False, [blocks[0]])[0]
    explicit_one, explicit_two = own_explicit(explicit_first, explicit_second, zx, sums)
    far, keep = add_pairs(pairs, zx, [sums])
    other_z = move_hist(far, 1, 0)
    near_blocks = cut_sums(sums, zx, [far])
    near_blocks = over_x(near_blocks)
    pred_one, sigma = predict(explicit_one, [keep, other_z], zx, [near_blocks[0]])

    rows = split_propagator(propagator, numbers(*sources, x), sums)
    begun, block = gathered(sigma)
    blocks = finish_first(rows[2:], [block], zx, span_late, begun)
    matrices = split_matrices([inverse_one, link, inverse_two], zx, [blocks[0]])
    parts = over_x(blocks)

    near = add_blocks(near_blocks, zx, [blocks[0]])
    near_other = move_hist(near, 1, 0)

    right = right_side(pred_one, parts, zx)
    moved, kept, *pieces = solve(
        right, move_hist(right, 1, 0), matrices, explicit_two, near, near_other, zx
    )
    begun, block = gathered(moved)
    pieces = over_x(pieces)
    blocks = finish_second(rows[2:], [block], zx, span_late, begun, kept)
    return tuple(last_rows(pieces, over_x(blocks), zx))


def solution(mesh):
    return jax.shard_map(
        shards,
        mesh=mesh,
        in_specs=(
            P("hist", "tcol"),
            P(None, "hist"),
            P(None, "hist"),
            P(),
            P(None, "tcol"),
            P(),
            P(),
            P(None, "tcol"),
            P(None, "tcol"),
        ),
        out_specs=(P("hist", "tcol"), P("hist", "tcol")),
        check_vma=False,
    )
```

profile of v0, /device:TPU:1, one launch (start us, length us, event | category | flops | bytes accessed | tf_op | source)
XLA Modules:
  0.0 125.3 jit_solution(10303556728066501625)
XLA Ops:
  0.7 5.8 %collect.2 = (f32[2,256,128]{2,1,0:T(8,128)S(1)}, f32[2,256,128]{2,1,0:T(8,128)S(1)}, f32[2,256,128]{2,1,0:T(8,128)S(1)}, f32[2,256,128]{2,1,0:T(8,128)S(1)}) custom-call(s32[2]{0:T(128)S(1)} %pad_add_fusion.at, f32[2048,512]{1,0:T(8,128)} %hist_ref.3, f32[512,2048]{1,0:T(8,128)} %weight_ref.2), custom_call_target="tpu_custom_call" | custom-call | tf_op jit(solution)/shard_map/collect/pallas_call | solution.py:137
  6.5 3.6 %collective-permute-start = (f32[2,256,128]{2,1,0:T(8,128)S(1)}, f32[2,256,128]{2,1,0:T(8,128)S(1)}, u32[]{:S(2)}, u32[]{:S(2)}) collective-permute-start(f32[2,256,128]{2,1,0:T(8,128)S(1)} %get-tuple-element.50), channel_id=1, source_target_pairs={{0,32},{16,48},{32,0},{48,16},{64,96},{80,112},{96,64},{112,80},{1... | collective-permute-start | bytes 786440 | tf_op jit(solution)/shard_map/ppermute | solution.py:23
  10.5 2.4 %collective-permute-start.2 = (f32[2,256,128]{2,1,0:T(8,128)S(1)}, f32[2,256,128]{2,1,0:T(8,128)S(1)}, u32[]{:S(2)}, u32[]{:S(2)}) collective-permute-start(f32[2,256,128]{2,1,0:T(8,128)S(1)} %get-tuple-element.52), channel_id=1, source_target_pairs={{0,48},{16,0},{32,16},{48,32},{64,112},{80,64},{96,80},{112,96},{1... | collective-permute-start | bytes 786440 | tf_op jit(solution)/shard_map/ppermute | solution.py:23
  12.8 5.7 %collect.3._.refs_4_.refs_0_ = f32[512,512]{1,0:T(8,128)S(1)} custom-call(s32[2]{0:T(128)S(1)} %pad_add_fusion.at, f32[2048,512]{1,0:T(8,128)} %hist_ref.3, f32[512,2048]{1,0:T(8,128)} %weight_ref.3, f32[2,256,128]{2,1,0:T(8,128)S(1)} %get-tuple-element.48.rest_0_.refs_0_), custom_call_target="tpu_custom_call" | custom-call | tf_op jit(solution)/shard_map/collect/pallas_call | solution.py:137
  18.5 4.0 %collective-permute-done.1.refs_2_ = f32[2,256,128]{2,1,0:T(8,128)S(1)} collective-permute-done((f32[2,256,128]{2,1,0:T(8,128)S(1)}, f32[2,256,128]{2,1,0:T(8,128)S(1)}, u32[]{:S(2)}, u32[]{:S(2)}) %collective-permute-start.1) | collective-permute-done | bytes 262176 | tf_op jit(solution)/shard_map/ppermute | solution.py:23
  23.2 3.9 %collective-permute-start.3 = (f32[256,128]{1,0:T(8,128)S(1)}, f32[256,128]{1,0:T(8,128)S(1)}, u32[]{:S(2)}, u32[]{:S(2)}) collective-permute-start(f32[256,128]{1,0:T(8,128)S(1)} %get-tuple-element.54.refs_1_), channel_id=1, source_target_pairs={{0,64},{16,80},{32,96},{48,112},{64,0},{80,16},{96,32},{112,48},{1... | collective-permute-start | bytes 393224 | tf_op jit(solution)/shard_map/ppermute | solution.py:23
  36.9 2.9 %split_propagator.1 = (bf16[1024,512]{1,0:T(8,128)(2,1)S(1)}, bf16[1024,512]{1,0:T(8,128)(2,1)S(1)}, bf16[1024,512]{1,0:T(8,128)(2,1)S(1)}, bf16[1024,512]{1,0:T(8,128)(2,1)S(1)}) custom-call(s32[17]{0:T(128)S(1)} %stack.80.at, f32[16,4,128,512]{3,2,1,0:T(8,128)} %bitcast.19, f32[512,512]{1,0:T(8,128)S(1)} %collect.3._.refs_4_.refs_0_), custom_call_target="tpu_custom_call" | custom-call | tf_op jit(solution)/shard_map/split_propagator/pallas_call | solution.py:175
  40.3 2.3 %collective-permute-done.4.refs_3_ = f32[256,128]{1,0:T(8,128)S(1)} collective-permute-done((f32[256,128]{1,0:T(8,128)S(1)}, f32[256,128]{1,0:T(8,128)S(1)}, u32[]{:S(2)}, u32[]{:S(2)}) %collective-permute-start.4) | collective-permute-done | bytes 131104 | tf_op jit(solution)/shard_map/ppermute | solution.py:31
  44.0 3.1 %collective-permute-start.12 = (f32[256,768]{1,0:T(8,128)S(1)}, f32[256,768]{1,0:T(8,128)S(1)}, u32[]{:S(2)}, u32[]{:S(2)}) collective-permute-start(f32[256,768]{1,0:T(8,128)S(1)} %get-tuple-element.64), channel_id=1, source_target_pairs={{0,1},{1,0},{2,3},{3,2},{4,5},{5,4},{6,7},{7,6},{8,9},{9,8},{10,11... | collective-permute-start | bytes 2359304 | tf_op jit(solution)/shard_map/ppermute | solution.py:35
  48.0 2.9 %collective-permute-done.7.refs_3_ = f32[256,128]{1,0:T(8,128)S(1)} collective-permute-done((f32[256,128]{1,0:T(8,128)S(1)}, f32[256,128]{1,0:T(8,128)S(1)}, u32[]{:S(2)}, u32[]{:S(2)}) %collective-permute-start.7) | collective-permute-done | bytes 131104 | tf_op jit(solution)/shard_map/ppermute | solution.py:31
  53.5 2.2 %collective-permute-start.11 = (f32[256,256]{1,0:T(8,128)S(1)}, f32[256,256]{1,0:T(8,128)S(1)}, u32[]{:S(2)}, u32[]{:S(2)}) collective-permute-start(f32[256,256]{1,0:T(8,128)S(1)} %get-tuple-element.63), channel_id=1, source_target_pairs={{0,1},{1,0},{2,3},{3,2},{4,5},{5,4},{6,7},{7,6},{8,9},{9,8},{10,11... | collective-permute-start | bytes 786440 | tf_op jit(solution)/shard_map/ppermute | solution.py:35
  65.1 2.5 %collective-permute-start.15 = (f32[256,128]{1,0:T(8,128)S(1)}, f32[256,128]{1,0:T(8,128)S(1)}, u32[]{:S(2)}, u32[]{:S(2)}) collective-permute-start(f32[256,128]{1,0:T(8,128)S(1)} %get-tuple-element.69), channel_id=1, source_target_pairs={{0,48},{16,0},{32,16},{48,32},{64,112},{80,64},{96,80},{112,96},{1... | collective-permute-start | bytes 393224 | tf_op jit(solution)/shard_map/ppermute | solution.py:23
  67.6 4.0 %collective-permute-done.18.refs_2_ = f32[512,128]{1,0:T(8,128)S(1)} collective-permute-done((f32[512,128]{1,0:T(8,128)S(1)}, f32[512,128]{1,0:T(8,128)S(1)}, u32[]{:S(2)}, u32[]{:S(2)}) %collective-permute-start.18) | collective-permute-done | bytes 262176 | tf_op jit(solution)/shard_map/ppermute | solution.py:23
  72.2 3.4 %collective-permute-start.20 = (f32[512,128]{1,0:T(8,128)S(1)}, f32[512,128]{1,0:T(8,128)S(1)}, u32[]{:S(2)}, u32[]{:S(2)}) collective-permute-start(f32[512,128]{1,0:T(8,128)S(1)} %shard_map.112.refs_3_), channel_id=1, source_target_pairs={{0,64},{16,80},{32,96},{48,112},{64,0},{80,16},{96,32},{112,48},{1... | collective-permute-start | bytes 786440 | tf_op jit(solution)/shard_map/ppermute | solution.py:23
  77.3 3.4 %collective-permute-start.16 = (f32[256,128]{1,0:T(8,128)S(1)}, f32[256,128]{1,0:T(8,128)S(1)}, u32[]{:S(2)}, u32[]{:S(2)}) collective-permute-start(f32[256,128]{1,0:T(8,128)S(1)} %shard_map.111.refs_0_), channel_id=1, source_target_pairs={{0,64},{16,80},{32,96},{48,112},{64,0},{80,16},{96,32},{112,48},{1... | collective-permute-start | bytes 393224 | tf_op jit(solution)/shard_map/ppermute | solution.py:23
  81.7 3.1 %collective-permute-done.16.refs_1_ = f32[256,128]{1,0:T(8,128)S(1)} collective-permute-done((f32[256,128]{1,0:T(8,128)S(1)}, f32[256,128]{1,0:T(8,128)S(1)}, u32[]{:S(2)}, u32[]{:S(2)}) %collective-permute-start.16) | collective-permute-done | bytes 131104 | tf_op jit(solution)/shard_map/ppermute | solution.py:23
  84.8 2.0 %shard_map.114 = (f32[256,128]{1,0:T(8,128)S(1)}, f32[256,128]{1,0:T(8,128)S(1)}, f32[64,128]{1,0:T(8,128)S(1)}, f32[64,128]{1,0:T(8,128)S(1)}, f32[64,128]{1,0:T(8,128)S(1)}, /*index=5*/f32[64,128]{1,0:T(8,128)S(1)}) custom-call(s32[2]{0:T(128)S(1)} %pad_add_fusion.at, f32[256,128]{1,0:T(8,128)S(1)} %shard_map.111.refs_0_, ...), custom_call_target="tpu_custom_call" | custom-call | tf_op jit(solution)/shard_map/pallas_call | solution.py:78
  87.3 3.5 %collective-permute-start.26 = (f32[256,128]{1,0:T(8,128)S(1)}, f32[256,128]{1,0:T(8,128)S(1)}, u32[]{:S(2)}, u32[]{:S(2)}) collective-permute-start(f32[256,128]{1,0:T(8,128)S(1)} %get-tuple-element.84.refs_2_), channel_id=1, source_target_pairs={{0,10},{1,15},{2,12},{3,9},{4,14},{5,11},{6,8},{7,13},{8,2},{9,7},... | collective-permute-start | bytes 393224 | tf_op jit(solution)/shard_map/ppermute | solution.py:31
  92.5 2.9 %collective-permute-done.28.refs_5_ = f32[256,128]{1,0:T(8,128)S(1)} collective-permute-done((f32[256,128]{1,0:T(8,128)S(1)}, f32[256,128]{1,0:T(8,128)S(1)}, u32[]{:S(2)}, u32[]{:S(2)}) %collective-permute-start.28) | collective-permute-done | bytes 131104 | tf_op jit(solution)/shard_map/ppermute | solution.py:31
  97.6 2.3 %collective-permute-start.32 = (f32[256,768]{1,0:T(8,128)S(1)}, f32[256,768]{1,0:T(8,128)S(1)}, u32[]{:S(2)}, u32[]{:S(2)}) collective-permute-start(f32[256,768]{1,0:T(8,128)S(1)} %get-tuple-element.87), channel_id=1, source_target_pairs={{0,1},{1,0},{2,3},{3,2},{4,5},{5,4},{6,7},{7,6},{8,9},{9,8},{10,11... | collective-permute-start | bytes 2359304 | tf_op jit(solution)/shard_map/ppermute | solution.py:35
  101.4 2.3 %collective-permute-done.27.refs_3_ = f32[256,128]{1,0:T(8,128)S(1)} collective-permute-done((f32[256,128]{1,0:T(8,128)S(1)}, f32[256,128]{1,0:T(8,128)S(1)}, u32[]{:S(2)}, u32[]{:S(2)}) %collective-permute-start.27) | collective-permute-done | bytes 131104 | tf_op jit(solution)/shard_map/ppermute | solution.py:31
  106.3 2.2 %collective-permute-start.31 = (f32[256,256]{1,0:T(8,128)S(1)}, f32[256,256]{1,0:T(8,128)S(1)}, u32[]{:S(2)}, u32[]{:S(2)}) collective-permute-start(f32[256,256]{1,0:T(8,128)S(1)} %get-tuple-element.86), channel_id=1, source_target_pairs={{0,1},{1,0},{2,3},{3,2},{4,5},{5,4},{6,7},{7,6},{8,9},{9,8},{10,11... | collective-permute-start | bytes 786440 | tf_op jit(solution)/shard_map/ppermute | solution.py:35
  116.5 4.0 %collective-permute-done.21.refs_1_ = f32[64,128]{1,0:T(8,128)S(1)} collective-permute-done((f32[64,128]{1,0:T(8,128)S(1)}, f32[64,128]{1,0:T(8,128)S(1)}, u32[]{:S(2)}, u32[]{:S(2)}) %collective-permute-start.21) | collective-permute-done | bytes 32800 | tf_op jit(solution)/shard_map/ppermute | solution.py:23
  120.5 2.4 %collective-permute-start.23 = (f32[64,128]{1,0:T(8,128)S(1)}, f32[64,128]{1,0:T(8,128)S(1)}, u32[]{:S(2)}, u32[]{:S(2)}) collective-permute-start(f32[64,128]{1,0:T(8,128)S(1)} %get-tuple-element.83), channel_id=1, source_target_pairs={{0,48},{16,0},{32,16},{48,32},{64,112},{80,64},{96,80},{112,96},{1... | collective-permute-start | bytes 98312 | tf_op jit(solution)/shard_map/ppermute | solution.py:23
  (76 shorter events, 47.6 us)
Async XLA Ops:
  6.5 12.0 %collective-permute-start = (f32[2,256,128]{2,1,0:T(8,128)S(1)}, f32[2,256,128]{2,1,0:T(8,128)S(1)}, u32[]{:S(2)}, u32[]{:S(2)}) collective-permute-start(f32[2,256,128]{2,1,0:T(8,128)S(1)} %get-tuple-element.50), channel_id=1, source_target_pairs={{0,32},{16,48},{32,0},{48,16},{64,96},{80,112},{96,64},{112,80},{1... | collective-permute-start | bytes 786440 | tf_op jit(solution)/shard_map/ppermute | solution.py:23
  10.2 12.4 %collective-permute-start.1 = (f32[2,256,128]{2,1,0:T(8,128)S(1)}, f32[2,256,128]{2,1,0:T(8,128)S(1)}, u32[]{:S(2)}, u32[]{:S(2)}) collective-permute-start(f32[2,256,128]{2,1,0:T(8,128)S(1)} %get-tuple-element.51), channel_id=1, source_target_pairs={{0,16},{16,32},{32,48},{48,0},{64,80},{80,96},{96,112},{112,64},{1... | collective-permute-start | bytes 786440 | tf_op jit(solution)/shard_map/ppermute | solution.py:23
  10.5 12.1 %collective-permute-start.2 = (f32[2,256,128]{2,1,0:T(8,128)S(1)}, f32[2,256,128]{2,1,0:T(8,128)S(1)}, u32[]{:S(2)}, u32[]{:S(2)}) collective-permute-start(f32[2,256,128]{2,1,0:T(8,128)S(1)} %get-tuple-element.52), channel_id=1, source_target_pairs={{0,48},{16,0},{32,16},{48,32},{64,112},{80,64},{96,80},{112,96},{1... | collective-permute-start | bytes 786440 | tf_op jit(solution)/shard_map/ppermute | solution.py:23
  23.2 7.2 %collective-permute-start.3 = (f32[256,128]{1,0:T(8,128)S(1)}, f32[256,128]{1,0:T(8,128)S(1)}, u32[]{:S(2)}, u32[]{:S(2)}) collective-permute-start(f32[256,128]{1,0:T(8,128)S(1)} %get-tuple-element.54.refs_1_), channel_id=1, source_target_pairs={{0,64},{16,80},{32,96},{48,112},{64,0},{80,16},{96,32},{112,48},{1... | collective-permute-start | bytes 393224 | tf_op jit(solution)/shard_map/ppermute | solution.py:23
  30.9 8.8 %collective-permute-start.10 = (f32[256,128]{1,0:T(8,128)S(1)}, f32[256,128]{1,0:T(8,128)S(1)}, u32[]{:S(2)}, u32[]{:S(2)}) collective-permute-start(f32[256,128]{1,0:T(8,128)S(1)} %get-tuple-element.61.refs_2_), channel_id=1, source_target_pairs={{0,8},{1,9},{2,10},{3,11},{4,12},{5,13},{6,14},{7,15},{8,0},{9,1},... | collective-permute-start | bytes 393224 | tf_op jit(solution)/shard_map/ppermute | solution.py:31
  31.7 8.0 %collective-permute-start.9 = (f32[256,128]{1,0:T(8,128)S(1)}, f32[256,128]{1,0:T(8,128)S(1)}, u32[]{:S(2)}, u32[]{:S(2)}) collective-permute-start(f32[256,128]{1,0:T(8,128)S(1)} %get-tuple-element.61.refs_2_), channel_id=1, source_target_pairs={{0,6},{1,3},{2,0},{3,5},{4,2},{5,7},{6,4},{7,1},{8,14},{9,11},{10,... | collective-permute-start | bytes 393224 | tf_op jit(solution)/shard_map/ppermute | solution.py:31
  33.0 6.8 %collective-permute-start.8 = (f32[256,128]{1,0:T(8,128)S(1)}, f32[256,128]{1,0:T(8,128)S(1)}, u32[]{:S(2)}, u32[]{:S(2)}) collective-permute-start(f32[256,128]{1,0:T(8,128)S(1)} %get-tuple-element.61.refs_2_), channel_id=1, source_target_pairs={{0,14},{1,11},{2,8},{3,13},{4,10},{5,15},{6,12},{7,9},{8,6},{9,3},... | collective-permute-start | bytes 393224 | tf_op jit(solution)/shard_map/ppermute | solution.py:31
  44.0 15.9 %collective-permute-start.12 = (f32[256,768]{1,0:T(8,128)S(1)}, f32[256,768]{1,0:T(8,128)S(1)}, u32[]{:S(2)}, u32[]{:S(2)}) collective-permute-start(f32[256,768]{1,0:T(8,128)S(1)} %get-tuple-element.64), channel_id=1, source_target_pairs={{0,1},{1,0},{2,3},{3,2},{4,5},{5,4},{6,7},{7,6},{8,9},{9,8},{10,11... | collective-permute-start | bytes 2359304 | tf_op jit(solution)/shard_map/ppermute | solution.py:35
  53.5 7.7 %collective-permute-start.11 = (f32[256,256]{1,0:T(8,128)S(1)}, f32[256,256]{1,0:T(8,128)S(1)}, u32[]{:S(2)}, u32[]{:S(2)}) collective-permute-start(f32[256,256]{1,0:T(8,128)S(1)} %get-tuple-element.63), channel_id=1, source_target_pairs={{0,1},{1,0},{2,3},{3,2},{4,5},{5,4},{6,7},{7,6},{8,9},{9,8},{10,11... | collective-permute-start | bytes 786440 | tf_op jit(solution)/shard_map/ppermute | solution.py:35
  55.7 9.3 %collective-permute-start.17 = (f32[512,128]{1,0:T(8,128)S(1)}, f32[512,128]{1,0:T(8,128)S(1)}, u32[]{:S(2)}, u32[]{:S(2)}) collective-permute-start(f32[512,128]{1,0:T(8,128)S(1)} %get-tuple-element.71), channel_id=1, source_target_pairs={{0,32},{16,48},{32,0},{48,16},{64,96},{80,112},{96,64},{112,80},{1... | collective-permute-start | bytes 786440 | tf_op jit(solution)/shard_map/ppermute | solution.py:23
  57.2 14.3 %collective-permute-start.18 = (f32[512,128]{1,0:T(8,128)S(1)}, f32[512,128]{1,0:T(8,128)S(1)}, u32[]{:S(2)}, u32[]{:S(2)}) collective-permute-start(f32[512,128]{1,0:T(8,128)S(1)} %get-tuple-element.72), channel_id=1, source_target_pairs={{0,16},{16,32},{32,48},{48,0},{64,80},{80,96},{96,112},{112,64},{1... | collective-permute-start | bytes 786440 | tf_op jit(solution)/shard_map/ppermute | solution.py:23
  58.8 12.7 %collective-permute-start.19 = (f32[512,128]{1,0:T(8,128)S(1)}, f32[512,128]{1,0:T(8,128)S(1)}, u32[]{:S(2)}, u32[]{:S(2)}) collective-permute-start(f32[512,128]{1,0:T(8,128)S(1)} %get-tuple-element.73), channel_id=1, source_target_pairs={{0,48},{16,0},{32,16},{48,32},{64,112},{80,64},{96,80},{112,96},{1... | collective-permute-start | bytes 786440 | tf_op jit(solution)/shard_map/ppermute | solution.py:23
  62.2 13.3 %collective-permute-start.13 = (f32[256,128]{1,0:T(8,128)S(1)}, f32[256,128]{1,0:T(8,128)S(1)}, u32[]{:S(2)}, u32[]{:S(2)}) collective-permute-start(f32[256,128]{1,0:T(8,128)S(1)} %get-tuple-element.67), channel_id=1, source_target_pairs={{0,32},{16,48},{32,0},{48,16},{64,96},{80,112},{96,64},{112,80},{1... | collective-permute-start | bytes 393224 | tf_op jit(solution)/shard_map/ppermute | solution.py:23
  63.0 13.7 %collective-permute-start.14 = (f32[256,128]{1,0:T(8,128)S(1)}, f32[256,128]{1,0:T(8,128)S(1)}, u32[]{:S(2)}, u32[]{:S(2)}) collective-permute-start(f32[256,128]{1,0:T(8,128)S(1)} %get-tuple-element.68), channel_id=1, source_target_pairs={{0,16},{16,32},{32,48},{48,0},{64,80},{80,96},{96,112},{112,64},{1... | collective-permute-start | bytes 393224 | tf_op jit(solution)/shard_map/ppermute | solution.py:23
  65.1 11.7 %collective-permute-start.15 = (f32[256,128]{1,0:T(8,128)S(1)}, f32[256,128]{1,0:T(8,128)S(1)}, u32[]{:S(2)}, u32[]{:S(2)}) collective-permute-start(f32[256,128]{1,0:T(8,128)S(1)} %get-tuple-element.69), channel_id=1, source_target_pairs={{0,48},{16,0},{32,16},{48,32},{64,112},{80,64},{96,80},{112,96},{1... | collective-permute-start | bytes 393224 | tf_op jit(solution)/shard_map/ppermute | solution.py:23
  72.2 12.6 %collective-permute-start.20 = (f32[512,128]{1,0:T(8,128)S(1)}, f32[512,128]{1,0:T(8,128)S(1)}, u32[]{:S(2)}, u32[]{:S(2)}) collective-permute-start(f32[512,128]{1,0:T(8,128)S(1)} %shard_map.112.refs_3_), channel_id=1, source_target_pairs={{0,64},{16,80},{32,96},{48,112},{64,0},{80,16},{96,32},{112,48},{1... | collective-permute-start | bytes 786440 | tf_op jit(solution)/shard_map/ppermute | solution.py:23
  77.3 7.5 %collective-permute-start.16 = (f32[256,128]{1,0:T(8,128)S(1)}, f32[256,128]{1,0:T(8,128)S(1)}, u32[]{:S(2)}, u32[]{:S(2)}) collective-permute-start(f32[256,128]{1,0:T(8,128)S(1)} %shard_map.111.refs_0_), channel_id=1, source_target_pairs={{0,64},{16,80},{32,96},{48,112},{64,0},{80,16},{96,32},{112,48},{1... | collective-permute-start | bytes 393224 | tf_op jit(solution)/shard_map/ppermute | solution.py:23
  87.0 8.4 %collective-permute-start.28 = (f32[256,128]{1,0:T(8,128)S(1)}, f32[256,128]{1,0:T(8,128)S(1)}, u32[]{:S(2)}, u32[]{:S(2)}) collective-permute-start(f32[256,128]{1,0:T(8,128)S(1)} %get-tuple-element.84.refs_2_), channel_id=1, source_target_pairs={{0,14},{1,11},{2,8},{3,13},{4,10},{5,15},{6,12},{7,9},{8,6},{9,3},... | collective-permute-start | bytes 393224 | tf_op jit(solution)/shard_map/ppermute | solution.py:31
  87.3 8.1 %collective-permute-start.26 = (f32[256,128]{1,0:T(8,128)S(1)}, f32[256,128]{1,0:T(8,128)S(1)}, u32[]{:S(2)}, u32[]{:S(2)}) collective-permute-start(f32[256,128]{1,0:T(8,128)S(1)} %get-tuple-element.84.refs_2_), channel_id=1, source_target_pairs={{0,10},{1,15},{2,12},{3,9},{4,14},{5,11},{6,8},{7,13},{8,2},{9,7},... | collective-permute-start | bytes 393224 | tf_op jit(solution)/shard_map/ppermute | solution.py:31
  97.6 10.9 %collective-permute-start.32 = (f32[256,768]{1,0:T(8,128)S(1)}, f32[256,768]{1,0:T(8,128)S(1)}, u32[]{:S(2)}, u32[]{:S(2)}) collective-permute-start(f32[256,768]{1,0:T(8,128)S(1)} %get-tuple-element.87), channel_id=1, source_target_pairs={{0,1},{1,0},{2,3},{3,2},{4,5},{5,4},{6,7},{7,6},{8,9},{9,8},{10,11... | collective-permute-start | bytes 2359304 | tf_op jit(solution)/shard_map/ppermute | solution.py:35
  110.8 13.1 %collective-permute-start.33 = (f32[64,512]{1,0:T(8,128)S(1)}, f32[64,512]{1,0:T(8,128)S(1)}, u32[]{:S(2)}, u32[]{:S(2)}) collective-permute-start(f32[64,512]{1,0:T(8,128)S(1)} %get-tuple-element.91), channel_id=1, source_target_pairs={{0,32},{16,48},{32,0},{48,16},{64,96},{80,112},{96,64},{112,80},{1... | collective-permute-start | bytes 393224 | tf_op jit(solution)/shard_map/ppermute | solution.py:23
  112.2 11.7 %collective-permute-start.34 = (f32[64,512]{1,0:T(8,128)S(1)}, f32[64,512]{1,0:T(8,128)S(1)}, u32[]{:S(2)}, u32[]{:S(2)}) collective-permute-start(f32[64,512]{1,0:T(8,128)S(1)} %get-tuple-element.92), channel_id=1, source_target_pairs={{0,16},{16,32},{32,48},{48,0},{64,80},{80,96},{96,112},{112,64},{1... | collective-permute-start | bytes 393224 | tf_op jit(solution)/shard_map/ppermute | solution.py:23
  113.9 10.0 %collective-permute-start.35 = (f32[64,512]{1,0:T(8,128)S(1)}, f32[64,512]{1,0:T(8,128)S(1)}, u32[]{:S(2)}, u32[]{:S(2)}) collective-permute-start(f32[64,512]{1,0:T(8,128)S(1)} %get-tuple-element.93), channel_id=1, source_target_pairs={{0,48},{16,0},{32,16},{48,32},{64,112},{80,64},{96,80},{112,96},{1... | collective-permute-start | bytes 393224 | tf_op jit(solution)/shard_map/ppermute | solution.py:23
  115.7 7.2 %collective-permute-start.22 = (f32[64,128]{1,0:T(8,128)S(1)}, f32[64,128]{1,0:T(8,128)S(1)}, u32[]{:S(2)}, u32[]{:S(2)}) collective-permute-start(f32[64,128]{1,0:T(8,128)S(1)} %get-tuple-element.82), channel_id=1, source_target_pairs={{0,16},{16,32},{32,48},{48,0},{64,80},{80,96},{96,112},{112,64},{1... | collective-permute-start | bytes 98312 | tf_op jit(solution)/shard_map/ppermute | solution.py:23
  (15 other events, 120.7 us)
where the time goes:
time: 127 us; the launch traced here: 125 us
  starting transfers between devices  56.6 us (45%)
  waiting for transfers between devices  35.3 us (28%)
  Pallas kernels  32.3 us (25%)
    ppermute x18, starting transfers between devices, move_hist(): return lax.ppermute(value, 'hist', pairs)  33.4 us
    ppermute x18, waiting for transfers between devices, move_hist(): return lax.ppermute(value, 'hist', pairs)  19.5 us
    pallas_call x16, Pallas kernels, call(): pl.pallas_call(body, in_specs=[SCALARS] + [WHOLE] * len(inputs) + [UNREAD...  16.4 us
    ppermute x14, waiting for transfers between devices, move_tcol(): return lax.ppermute(value, 'tcol', [(i, target(i)) for i in range(16)])  15.8 us
    ppermute x14, starting transfers between devices, move_tcol(): return lax.ppermute(value, 'tcol', [(i, target(i)) for i in range(16)])  13.4 us
    pallas_call x2, Pallas kernels, collect(): pl.pallas_call(kernel, in_specs=[SCALARS, UNREAD, UNREAD] + [UNREAD] * n,...  11.5 us
    ppermute x4, starting transfers between devices, other_core(): return lax.ppermute(value, 'tcol', [(i, i ^ 1) for i in range(16)])  9.81 us
    pallas_call x1, Pallas kernels, split_propagator(): pl.pallas_call(kernel, in_specs=[SCALARS, UNREAD, UNREAD], out_specs=[WHO...  2.87 us
  transfers between devices with their start and end apart: 36, of which 18 were waited for; matrix products, arithmetic and copies ran while one was open for 0% of the time, Pallas kernels for 15%

commit v1 on v0

--- a/solution.py
+++ b/solution.py
@@ -183,34 +183,6 @@
     )(where, blocks, after)
 
 
-def own_explicit(explicit_one, explicit_two, where, after):
-    size = explicit_one.shape[0]
-
-    def kernel(at, first_ref, second_ref, _, first_out, second_out):
-        first_out[...] = first_ref[...]
-        second_out[...] = second_ref[...]
-
-    return pl.pallas_call(
-        kernel,
-        grid_spec=pltpu.PrefetchScalarGridSpec(
-            num_scalar_prefetch=1,
-            grid=(1,),
-            in_specs=[
-                pl.BlockSpec((size // 2, LANES), lambda i, at: (at[0], at[1])),
-                pl.BlockSpec((size, LANES), lambda i, at: (0, at[1])),
-                UNREAD,
-            ],
-            out_specs=[WHOLE] * 2,
-        ),
-        out_shape=[
-            jax.ShapeDtypeStruct((size // 2, LANES), F32),
-            jax.ShapeDtypeStruct((size, LANES), F32),
-        ],
-        name="own_explicit",
-        compiler_params=pltpu.CompilerParams(vmem_limit_bytes=4 << 20),
-    )(where, in_hbm(explicit_one), in_hbm(explicit_two), after)
-
-
 def split_matrices(matrices, where, after):
     size = matrices[0].shape[0]
     half = size // 2
@@ -225,12 +197,14 @@
 
 
 def predict(explicit, parts, where, after):
-    def kernel(at, *refs):
-        pred = total(refs[:-2])
+    half = explicit.shape[0] // 2
+
+    def kernel(at, explicit_ref, *refs):
+        pred = explicit_ref[rows_from(at[0] * half, half), lanes_from(at[1])] + total(refs[:-2])
         refs[-2][...] = pred
         refs[-1][...] = cubic_power(pred)
 
-    outs = [(explicit.shape, F32)] * 2
+    outs = [((half, LANES), F32)] * 2
     return call(kernel, outs, where, [explicit, *parts], after)
 
 
@@ -311,7 +285,7 @@
         right[rows_from(at[0] * half, half), :] = own_ref[...]
         right[rows_from((at[0] ^ 1) * half, half), :] = other_ref[...]
         first[...] = narrow_product((mats[0][...], mats[1][...]), split(right[...]))
-        pred = explicit_ref[...] + (near_ref[...] + far_ref[...])
+        pred = explicit_ref[:, lanes_from(at[1])] + (near_ref[...] + far_ref[...])
         pred = pred + narrow_product((mats[2][...], mats[3][...]), split(cubic_power(first[...])))
         both = jnp.concatenate([step_size * cubic_power(pred), pred], axis=1)
         solved = product((mats[4][...], mats[5][...]), split(both))
@@ -398,12 +372,13 @@
     blocks = collect(history, memory_weight_first, zx, True)
     pairs = over_x(blocks)
     sums = collect(history, memory_weight_second, zx, False, [blocks[0]])[0]
-    explicit_one, explicit_two = own_explicit(explicit_first, explicit_second, zx, sums)
     far, keep = add_pairs(pairs, zx, [sums])
     other_z = move_hist(far, 1, 0)
     near_blocks = cut_sums(sums, zx, [far])
-    near_blocks = over_x(near_blocks)
-    pred_one, sigma = predict(explicit_one, [keep, other_z], zx, [near_blocks[0]])
+    near_a = move_hist(near_blocks[2], 0, 2)
+    near_b = [move_hist(near_blocks[d], 0, d) for d in (1, 3)]
+    pred_one, sigma = predict(explicit_first, [keep, other_z], zx, [near_blocks[0]])
+    near_blocks = [near_blocks[0], near_a, *near_b]
 
     rows = split_propagator(propagator, numbers(*sources, x), sums)
     begun, block = gathered(sigma)
@@ -416,7 +391,7 @@
 
     right = right_side(pred_one, parts, zx)
     moved, kept, *pieces = solve(
-        right, move_hist(right, 1, 0), matrices, explicit_two, near, near_other, zx
+        right, move_hist(right, 1, 0), matrices, explicit_second, near, near_other, zx
     )
     begun, block = gathered(moved)
     pieces = over_x(pieces)

time: 127 us -> 127 us (level)
  Pallas kernels: 32.3 us -> 30.7 us
  waiting for transfers between devices: 35.3 us -> 36.8 us
    pallas_call x1 -> x0, Pallas kernels: 1.59 us -> none  [own_explicit(): pl.pallas_call(kernel, grid_spec=pltpu.PrefetchScalarGridSpec(num_scalar_...]
    ppermute x18, waiting for transfers between devices: 19.5 us -> 21 us  [move_hist(): return lax.ppermute(value, 'hist', pairs)]
  transfers between devices with their start and end apart: 36 -> 36, of which waited for: 18 -> 18; matrix products, arithmetic and copies ran while one was open for 0% -> 0% of each run, Pallas kernels for 15% -> 13%
where the time goes in v1:
time: 127 us; the launch traced here: 125 us
  starting transfers between devices  56.7 us (45%)
  waiting for transfers between devices  36.8 us (29%)
  Pallas kernels  30.7 us (24%)
    ppermute x18, starting transfers between devices, move_hist(): return lax.ppermute(value, 'hist', pairs)  33.4 us
    ppermute x18, waiting for transfers between devices, move_hist(): return lax.ppermute(value, 'hist', pairs)  21 us
    pallas_call x16, Pallas kernels, call(): pl.pallas_call(body, in_specs=[SCALARS] + [WHOLE] * len(inputs) + [UNREAD...  16.4 us
    ppermute x14, waiting for transfers between devices, move_tcol(): return lax.ppermute(value, 'tcol', [(i, target(i)) for i in range(16)])  15.8 us
    ppermute x14, starting transfers between devices, move_tcol(): return lax.ppermute(value, 'tcol', [(i, target(i)) for i in range(16)])  13.4 us
    pallas_call x2, Pallas kernels, collect(): pl.pallas_call(kernel, in_specs=[SCALARS, UNREAD, UNREAD] + [UNREAD] * n,...  11.5 us
    ppermute x4, starting transfers between devices, other_core(): return lax.ppermute(value, 'tcol', [(i, i ^ 1) for i in range(16)])  9.81 us
    pallas_call x1, Pallas kernels, split_propagator(): pl.pallas_call(kernel, in_specs=[SCALARS, UNREAD, UNREAD], out_specs=[WHO...  2.87 us
  transfers between devices with their start and end apart: 36, of which 18 were waited for; matrix products, arithmetic and copies ran while one was open for 0% of the time, Pallas kernels for 13%

profile of v1, /device:TPU:1, one launch (start us, length us, event | category | flops | bytes accessed | tf_op | source)
XLA Modules:
  0.0 125.3 jit_solution(10519306371162301934)
XLA Ops:
  0.7 5.8 %collect.2 = (f32[2,256,128]{2,1,0:T(8,128)S(1)}, f32[2,256,128]{2,1,0:T(8,128)S(1)}, f32[2,256,128]{2,1,0:T(8,128)S(1)}, f32[2,256,128]{2,1,0:T(8,128)S(1)}) custom-call(s32[2]{0:T(128)S(1)} %pad_add_fusion.at, f32[2048,512]{1,0:T(8,128)} %hist_ref.3, f32[512,2048]{1,0:T(8,128)} %weight_ref.2), custom_call_target="tpu_custom_call" | custom-call | tf_op jit(solution)/shard_map/collect/pallas_call | solution.py:137
  6.5 3.6 %collective-permute-start = (f32[2,256,128]{2,1,0:T(8,128)S(1)}, f32[2,256,128]{2,1,0:T(8,128)S(1)}, u32[]{:S(2)}, u32[]{:S(2)}) collective-permute-start(f32[2,256,128]{2,1,0:T(8,128)S(1)} %get-tuple-element.47), channel_id=1, source_target_pairs={{0,32},{16,48},{32,0},{48,16},{64,96},{80,112},{96,64},{112,80},{1... | collective-permute-start | bytes 786440 | tf_op jit(solution)/shard_map/ppermute | solution.py:23
  10.5 2.4 %collective-permute-start.2 = (f32[2,256,128]{2,1,0:T(8,128)S(1)}, f32[2,256,128]{2,1,0:T(8,128)S(1)}, u32[]{:S(2)}, u32[]{:S(2)}) collective-permute-start(f32[2,256,128]{2,1,0:T(8,128)S(1)} %get-tuple-element.49), channel_id=1, source_target_pairs={{0,48},{16,0},{32,16},{48,32},{64,112},{80,64},{96,80},{112,96},{1... | collective-permute-start | bytes 786440 | tf_op jit(solution)/shard_map/ppermute | solution.py:23
  12.8 5.7 %collect.3.refs_4_.refs_0_._ = f32[512,512]{1,0:T(8,128)S(1)} custom-call(s32[2]{0:T(128)S(1)} %pad_add_fusion.at, f32[2048,512]{1,0:T(8,128)} %hist_ref.3, f32[512,2048]{1,0:T(8,128)} %weight_ref.3, f32[2,256,128]{2,1,0:T(8,128)S(1)} %get-tuple-element.46.rest_0_.refs_0_), custom_call_target="tpu_custom_call" | custom-call | tf_op jit(solution)/shard_map/collect/pallas_call | solution.py:137
  18.5 4.0 %collective-permute-done.1.refs_2_ = f32[2,256,128]{2,1,0:T(8,128)S(1)} collective-permute-done((f32[2,256,128]{2,1,0:T(8,128)S(1)}, f32[2,256,128]{2,1,0:T(8,128)S(1)}, u32[]{:S(2)}, u32[]{:S(2)}) %collective-permute-start.1) | collective-permute-done | bytes 262176 | tf_op jit(solution)/shard_map/ppermute | solution.py:23
  23.2 3.9 %collective-permute-start.3 = (f32[256,128]{1,0:T(8,128)S(1)}, f32[256,128]{1,0:T(8,128)S(1)}, u32[]{:S(2)}, u32[]{:S(2)}) collective-permute-start(f32[256,128]{1,0:T(8,128)S(1)} %get-tuple-element.51.refs_1_), channel_id=1, source_target_pairs={{0,64},{16,80},{32,96},{48,112},{64,0},{80,16},{96,32},{112,48},{1... | collective-permute-start | bytes 393224 | tf_op jit(solution)/shard_map/ppermute | solution.py:23
  27.8 2.6 %collective-permute-done.3.refs_2_ = f32[256,128]{1,0:T(8,128)S(1)} collective-permute-done((f32[256,128]{1,0:T(8,128)S(1)}, f32[256,128]{1,0:T(8,128)S(1)}, u32[]{:S(2)}, u32[]{:S(2)}) %collective-permute-start.3) | collective-permute-done | bytes 131104 | tf_op jit(solution)/shard_map/ppermute | solution.py:23
  36.9 2.9 %split_propagator.1 = (bf16[1024,512]{1,0:T(8,128)(2,1)S(1)}, bf16[1024,512]{1,0:T(8,128)(2,1)S(1)}, bf16[1024,512]{1,0:T(8,128)(2,1)S(1)}, bf16[1024,512]{1,0:T(8,128)(2,1)S(1)}) custom-call(s32[17]{0:T(128)S(1)} %stack.80.at, f32[16,4,128,512]{3,2,1,0:T(8,128)} %bitcast.19, f32[512,512]{1,0:T(8,128)S(1)} %collect.3.refs_4_.refs_0_._), custom_call_target="tpu_custom_call" | custom-call | tf_op jit(solution)/shard_map/split_propagator/pallas_call | solution.py:175
  40.3 2.3 %collective-permute-done.4.refs_3_ = f32[256,128]{1,0:T(8,128)S(1)} collective-permute-done((f32[256,128]{1,0:T(8,128)S(1)}, f32[256,128]{1,0:T(8,128)S(1)}, u32[]{:S(2)}, u32[]{:S(2)}) %collective-permute-start.4) | collective-permute-done | bytes 131104 | tf_op jit(solution)/shard_map/ppermute | solution.py:31
  44.0 3.1 %collective-permute-start.12 = (f32[256,768]{1,0:T(8,128)S(1)}, f32[256,768]{1,0:T(8,128)S(1)}, u32[]{:S(2)}, u32[]{:S(2)}) collective-permute-start(f32[256,768]{1,0:T(8,128)S(1)} %get-tuple-element.61), channel_id=1, source_target_pairs={{0,1},{1,0},{2,3},{3,2},{4,5},{5,4},{6,7},{7,6},{8,9},{9,8},{10,11... | collective-permute-start | bytes 2359304 | tf_op jit(solution)/shard_map/ppermute | solution.py:35
  48.0 2.9 %collective-permute-done.7.refs_3_ = f32[256,128]{1,0:T(8,128)S(1)} collective-permute-done((f32[256,128]{1,0:T(8,128)S(1)}, f32[256,128]{1,0:T(8,128)S(1)}, u32[]{:S(2)}, u32[]{:S(2)}) %collective-permute-start.7) | collective-permute-done | bytes 131104 | tf_op jit(solution)/shard_map/ppermute | solution.py:31
  53.5 2.2 %collective-permute-start.11 = (f32[256,256]{1,0:T(8,128)S(1)}, f32[256,256]{1,0:T(8,128)S(1)}, u32[]{:S(2)}, u32[]{:S(2)}) collective-permute-start(f32[256,256]{1,0:T(8,128)S(1)} %get-tuple-element.60), channel_id=1, source_target_pairs={{0,1},{1,0},{2,3},{3,2},{4,5},{5,4},{6,7},{7,6},{8,9},{9,8},{10,11... | collective-permute-start | bytes 786440 | tf_op jit(solution)/shard_map/ppermute | solution.py:35
  65.1 2.5 %collective-permute-start.15 = (f32[256,128]{1,0:T(8,128)S(1)}, f32[256,128]{1,0:T(8,128)S(1)}, u32[]{:S(2)}, u32[]{:S(2)}) collective-permute-start(f32[256,128]{1,0:T(8,128)S(1)} %get-tuple-element.66), channel_id=1, source_target_pairs={{0,48},{16,0},{32,16},{48,32},{64,112},{80,64},{96,80},{112,96},{1... | collective-permute-start | bytes 393224 | tf_op jit(solution)/shard_map/ppermute | solution.py:23
  67.6 4.0 %collective-permute-done.18.refs_2_ = f32[512,128]{1,0:T(8,128)S(1)} collective-permute-done((f32[512,128]{1,0:T(8,128)S(1)}, f32[512,128]{1,0:T(8,128)S(1)}, u32[]{:S(2)}, u32[]{:S(2)}) %collective-permute-start.18) | collective-permute-done | bytes 262176 | tf_op jit(solution)/shard_map/ppermute | solution.py:23
  72.2 3.4 %collective-permute-start.20 = (f32[512,128]{1,0:T(8,128)S(1)}, f32[512,128]{1,0:T(8,128)S(1)}, u32[]{:S(2)}, u32[]{:S(2)}) collective-permute-start(f32[512,128]{1,0:T(8,128)S(1)} %shard_map.112.refs_3_), channel_id=1, source_target_pairs={{0,64},{16,80},{32,96},{48,112},{64,0},{80,16},{96,32},{112,48},{1... | collective-permute-start | bytes 786440 | tf_op jit(solution)/shard_map/ppermute | solution.py:23
  77.3 3.4 %collective-permute-start.16 = (f32[256,128]{1,0:T(8,128)S(1)}, f32[256,128]{1,0:T(8,128)S(1)}, u32[]{:S(2)}, u32[]{:S(2)}) collective-permute-start(f32[256,128]{1,0:T(8,128)S(1)} %shard_map.111.refs_0_), channel_id=1, source_target_pairs={{0,64},{16,80},{32,96},{48,112},{64,0},{80,16},{96,32},{112,48},{1... | collective-permute-start | bytes 393224 | tf_op jit(solution)/shard_map/ppermute | solution.py:23
  81.7 3.1 %collective-permute-done.16.refs_1_ = f32[256,128]{1,0:T(8,128)S(1)} collective-permute-done((f32[256,128]{1,0:T(8,128)S(1)}, f32[256,128]{1,0:T(8,128)S(1)}, u32[]{:S(2)}, u32[]{:S(2)}) %collective-permute-start.16) | collective-permute-done | bytes 131104 | tf_op jit(solution)/shard_map/ppermute | solution.py:23
  87.3 3.5 %collective-permute-start.26 = (f32[256,128]{1,0:T(8,128)S(1)}, f32[256,128]{1,0:T(8,128)S(1)}, u32[]{:S(2)}, u32[]{:S(2)}) collective-permute-start(f32[256,128]{1,0:T(8,128)S(1)} %get-tuple-element.80.refs_2_), channel_id=1, source_target_pairs={{0,10},{1,15},{2,12},{3,9},{4,14},{5,11},{6,8},{7,13},{8,2},{9,7},... | collective-permute-start | bytes 393224 | tf_op jit(solution)/shard_map/ppermute | solution.py:31
  92.5 2.9 %collective-permute-done.28.refs_5_ = f32[256,128]{1,0:T(8,128)S(1)} collective-permute-done((f32[256,128]{1,0:T(8,128)S(1)}, f32[256,128]{1,0:T(8,128)S(1)}, u32[]{:S(2)}, u32[]{:S(2)}) %collective-permute-start.28) | collective-permute-done | bytes 131104 | tf_op jit(solution)/shard_map/ppermute | solution.py:31
  97.6 2.3 %collective-permute-start.32 = (f32[256,768]{1,0:T(8,128)S(1)}, f32[256,768]{1,0:T(8,128)S(1)}, u32[]{:S(2)}, u32[]{:S(2)}) collective-permute-start(f32[256,768]{1,0:T(8,128)S(1)} %get-tuple-element.83), channel_id=1, source_target_pairs={{0,1},{1,0},{2,3},{3,2},{4,5},{5,4},{6,7},{7,6},{8,9},{9,8},{10,11... | collective-permute-start | bytes 2359304 | tf_op jit(solution)/shard_map/ppermute | solution.py:35
  101.4 2.3 %collective-permute-done.27.refs_3_ = f32[256,128]{1,0:T(8,128)S(1)} collective-permute-done((f32[256,128]{1,0:T(8,128)S(1)}, f32[256,128]{1,0:T(8,128)S(1)}, u32[]{:S(2)}, u32[]{:S(2)}) %collective-permute-start.27) | collective-permute-done | bytes 131104 | tf_op jit(solution)/shard_map/ppermute | solution.py:31
  106.3 2.2 %collective-permute-start.31 = (f32[256,256]{1,0:T(8,128)S(1)}, f32[256,256]{1,0:T(8,128)S(1)}, u32[]{:S(2)}, u32[]{:S(2)}) collective-permute-start(f32[256,256]{1,0:T(8,128)S(1)} %get-tuple-element.82), channel_id=1, source_target_pairs={{0,1},{1,0},{2,3},{3,2},{4,5},{5,4},{6,7},{7,6},{8,9},{9,8},{10,11... | collective-permute-start | bytes 786440 | tf_op jit(solution)/shard_map/ppermute | solution.py:35
  116.6 3.9 %collective-permute-done.21.refs_1_ = f32[64,128]{1,0:T(8,128)S(1)} collective-permute-done((f32[64,128]{1,0:T(8,128)S(1)}, f32[64,128]{1,0:T(8,128)S(1)}, u32[]{:S(2)}, u32[]{:S(2)}) %collective-permute-start.21) | collective-permute-done | bytes 32800 | tf_op jit(solution)/shard_map/ppermute | solution.py:23
  120.5 2.5 %collective-permute-start.23 = (f32[64,128]{1,0:T(8,128)S(1)}, f32[64,128]{1,0:T(8,128)S(1)}, u32[]{:S(2)}, u32[]{:S(2)}) collective-permute-start(f32[64,128]{1,0:T(8,128)S(1)} %get-tuple-element.79), channel_id=1, source_target_pairs={{0,48},{16,0},{32,16},{48,32},{64,112},{80,64},{96,80},{112,96},{1... | collective-permute-start | bytes 98312 | tf_op jit(solution)/shard_map/ppermute | solution.py:23
  (79 shorter events, 47.1 us)
Async XLA Ops:
  6.5 12.0 %collective-permute-start = (f32[2,256,128]{2,1,0:T(8,128)S(1)}, f32[2,256,128]{2,1,0:T(8,128)S(1)}, u32[]{:S(2)}, u32[]{:S(2)}) collective-permute-start(f32[2,256,128]{2,1,0:T(8,128)S(1)} %get-tuple-element.47), channel_id=1, source_target_pairs={{0,32},{16,48},{32,0},{48,16},{64,96},{80,112},{96,64},{112,80},{1... | collective-permute-start | bytes 786440 | tf_op jit(solution)/shard_map/ppermute | solution.py:23
  10.2 12.4 %collective-permute-start.1 = (f32[2,256,128]{2,1,0:T(8,128)S(1)}, f32[2,256,128]{2,1,0:T(8,128)S(1)}, u32[]{:S(2)}, u32[]{:S(2)}) collective-permute-start(f32[2,256,128]{2,1,0:T(8,128)S(1)} %get-tuple-element.48), channel_id=1, source_target_pairs={{0,16},{16,32},{32,48},{48,0},{64,80},{80,96},{96,112},{112,64},{1... | collective-permute-start | bytes 786440 | tf_op jit(solution)/shard_map/ppermute | solution.py:23
  10.5 12.1 %collective-permute-start.2 = (f32[2,256,128]{2,1,0:T(8,128)S(1)}, f32[2,256,128]{2,1,0:T(8,128)S(1)}, u32[]{:S(2)}, u32[]{:S(2)}) collective-permute-start(f32[2,256,128]{2,1,0:T(8,128)S(1)} %get-tuple-element.49), channel_id=1, source_target_pairs={{0,48},{16,0},{32,16},{48,32},{64,112},{80,64},{96,80},{112,96},{1... | collective-permute-start | bytes 786440 | tf_op jit(solution)/shard_map/ppermute | solution.py:23
  23.2 7.2 %collective-permute-start.3 = (f32[256,128]{1,0:T(8,128)S(1)}, f32[256,128]{1,0:T(8,128)S(1)}, u32[]{:S(2)}, u32[]{:S(2)}) collective-permute-start(f32[256,128]{1,0:T(8,128)S(1)} %get-tuple-element.51.refs_1_), channel_id=1, source_target_pairs={{0,64},{16,80},{32,96},{48,112},{64,0},{80,16},{96,32},{112,48},{1... | collective-permute-start | bytes 393224 | tf_op jit(solution)/shard_map/ppermute | solution.py:23
  30.9 8.8 %collective-permute-start.10 = (f32[256,128]{1,0:T(8,128)S(1)}, f32[256,128]{1,0:T(8,128)S(1)}, u32[]{:S(2)}, u32[]{:S(2)}) collective-permute-start(f32[256,128]{1,0:T(8,128)S(1)} %get-tuple-element.58.refs_2_), channel_id=1, source_target_pairs={{0,8},{1,9},{2,10},{3,11},{4,12},{5,13},{6,14},{7,15},{8,0},{9,1},... | collective-permute-start | bytes 393224 | tf_op jit(solution)/shard_map/ppermute | solution.py:31
  31.7 8.0 %collective-permute-start.9 = (f32[256,128]{1,0:T(8,128)S(1)}, f32[256,128]{1,0:T(8,128)S(1)}, u32[]{:S(2)}, u32[]{:S(2)}) collective-permute-start(f32[256,128]{1,0:T(8,128)S(1)} %get-tuple-element.58.refs_2_), channel_id=1, source_target_pairs={{0,6},{1,3},{2,0},{3,5},{4,2},{5,7},{6,4},{7,1},{8,14},{9,11},{10,... | collective-permute-start | bytes 393224 | tf_op jit(solution)/shard_map/ppermute | solution.py:31
  33.0 6.8 %collective-permute-start.8 = (f32[256,128]{1,0:T(8,128)S(1)}, f32[256,128]{1,0:T(8,128)S(1)}, u32[]{:S(2)}, u32[]{:S(2)}) collective-permute-start(f32[256,128]{1,0:T(8,128)S(1)} %get-tuple-element.58.refs_2_), channel_id=1, source_target_pairs={{0,14},{1,11},{2,8},{3,13},{4,10},{5,15},{6,12},{7,9},{8,6},{9,3},... | collective-permute-start | bytes 393224 | tf_op jit(solution)/shard_map/ppermute | solution.py:31
  44.0 15.9 %collective-permute-start.12 = (f32[256,768]{1,0:T(8,128)S(1)}, f32[256,768]{1,0:T(8,128)S(1)}, u32[]{:S(2)}, u32[]{:S(2)}) collective-permute-start(f32[256,768]{1,0:T(8,128)S(1)} %get-tuple-element.61), channel_id=1, source_target_pairs={{0,1},{1,0},{2,3},{3,2},{4,5},{5,4},{6,7},{7,6},{8,9},{9,8},{10,11... | collective-permute-start | bytes 2359304 | tf_op jit(solution)/shard_map/ppermute | solution.py:35
  53.5 7.7 %collective-permute-start.11 = (f32[256,256]{1,0:T(8,128)S(1)}, f32[256,256]{1,0:T(8,128)S(1)}, u32[]{:S(2)}, u32[]{:S(2)}) collective-permute-start(f32[256,256]{1,0:T(8,128)S(1)} %get-tuple-element.60), channel_id=1, source_target_pairs={{0,1},{1,0},{2,3},{3,2},{4,5},{5,4},{6,7},{7,6},{8,9},{9,8},{10,11... | collective-permute-start | bytes 786440 | tf_op jit(solution)/shard_map/ppermute | solution.py:35
  55.8 9.3 %collective-permute-start.17 = (f32[512,128]{1,0:T(8,128)S(1)}, f32[512,128]{1,0:T(8,128)S(1)}, u32[]{:S(2)}, u32[]{:S(2)}) collective-permute-start(f32[512,128]{1,0:T(8,128)S(1)} %get-tuple-element.67), channel_id=1, source_target_pairs={{0,32},{16,48},{32,0},{48,16},{64,96},{80,112},{96,64},{112,80},{1... | collective-permute-start | bytes 786440 | tf_op jit(solution)/shard_map/ppermute | solution.py:23
  57.2 14.3 %collective-permute-start.18 = (f32[512,128]{1,0:T(8,128)S(1)}, f32[512,128]{1,0:T(8,128)S(1)}, u32[]{:S(2)}, u32[]{:S(2)}) collective-permute-start(f32[512,128]{1,0:T(8,128)S(1)} %get-tuple-element.68), channel_id=1, source_target_pairs={{0,16},{16,32},{32,48},{48,0},{64,80},{80,96},{96,112},{112,64},{1... | collective-permute-start | bytes 786440 | tf_op jit(solution)/shard_map/ppermute | solution.py:23
  58.8 12.7 %collective-permute-start.19 = (f32[512,128]{1,0:T(8,128)S(1)}, f32[512,128]{1,0:T(8,128)S(1)}, u32[]{:S(2)}, u32[]{:S(2)}) collective-permute-start(f32[512,128]{1,0:T(8,128)S(1)} %get-tuple-element.69), channel_id=1, source_target_pairs={{0,48},{16,0},{32,16},{48,32},{64,112},{80,64},{96,80},{112,96},{1... | collective-permute-start | bytes 786440 | tf_op jit(solution)/shard_map/ppermute | solution.py:23
  62.2 13.3 %collective-permute-start.13 = (f32[256,128]{1,0:T(8,128)S(1)}, f32[256,128]{1,0:T(8,128)S(1)}, u32[]{:S(2)}, u32[]{:S(2)}) collective-permute-start(f32[256,128]{1,0:T(8,128)S(1)} %get-tuple-element.64), channel_id=1, source_target_pairs={{0,32},{16,48},{32,0},{48,16},{64,96},{80,112},{96,64},{112,80},{1... | collective-permute-start | bytes 393224 | tf_op jit(solution)/shard_map/ppermute | solution.py:23
  63.1 13.7 %collective-permute-start.14 = (f32[256,128]{1,0:T(8,128)S(1)}, f32[256,128]{1,0:T(8,128)S(1)}, u32[]{:S(2)}, u32[]{:S(2)}) collective-permute-start(f32[256,128]{1,0:T(8,128)S(1)} %get-tuple-element.65), channel_id=1, source_target_pairs={{0,16},{16,32},{32,48},{48,0},{64,80},{80,96},{96,112},{112,64},{1... | collective-permute-start | bytes 393224 | tf_op jit(solution)/shard_map/ppermute | solution.py:23
  65.1 11.7 %collective-permute-start.15 = (f32[256,128]{1,0:T(8,128)S(1)}, f32[256,128]{1,0:T(8,128)S(1)}, u32[]{:S(2)}, u32[]{:S(2)}) collective-permute-start(f32[256,128]{1,0:T(8,128)S(1)} %get-tuple-element.66), channel_id=1, source_target_pairs={{0,48},{16,0},{32,16},{48,32},{64,112},{80,64},{96,80},{112,96},{1... | collective-permute-start | bytes 393224 | tf_op jit(solution)/shard_map/ppermute | solution.py:23
  72.2 12.6 %collective-permute-start.20 = (f32[512,128]{1,0:T(8,128)S(1)}, f32[512,128]{1,0:T(8,128)S(1)}, u32[]{:S(2)}, u32[]{:S(2)}) collective-permute-start(f32[512,128]{1,0:T(8,128)S(1)} %shard_map.112.refs_3_), channel_id=1, source_target_pairs={{0,64},{16,80},{32,96},{48,112},{64,0},{80,16},{96,32},{112,48},{1... | collective-permute-start | bytes 786440 | tf_op jit(solution)/shard_map/ppermute | solution.py:23
  77.3 7.5 %collective-permute-start.16 = (f32[256,128]{1,0:T(8,128)S(1)}, f32[256,128]{1,0:T(8,128)S(1)}, u32[]{:S(2)}, u32[]{:S(2)}) collective-permute-start(f32[256,128]{1,0:T(8,128)S(1)} %shard_map.111.refs_0_), channel_id=1, source_target_pairs={{0,64},{16,80},{32,96},{48,112},{64,0},{80,16},{96,32},{112,48},{1... | collective-permute-start | bytes 393224 | tf_op jit(solution)/shard_map/ppermute | solution.py:23
  87.0 8.4 %collective-permute-start.28 = (f32[256,128]{1,0:T(8,128)S(1)}, f32[256,128]{1,0:T(8,128)S(1)}, u32[]{:S(2)}, u32[]{:S(2)}) collective-permute-start(f32[256,128]{1,0:T(8,128)S(1)} %get-tuple-element.80.refs_2_), channel_id=1, source_target_pairs={{0,14},{1,11},{2,8},{3,13},{4,10},{5,15},{6,12},{7,9},{8,6},{9,3},... | collective-permute-start | bytes 393224 | tf_op jit(solution)/shard_map/ppermute | solution.py:31
  87.3 8.1 %collective-permute-start.26 = (f32[256,128]{1,0:T(8,128)S(1)}, f32[256,128]{1,0:T(8,128)S(1)}, u32[]{:S(2)}, u32[]{:S(2)}) collective-permute-start(f32[256,128]{1,0:T(8,128)S(1)} %get-tuple-element.80.refs_2_), channel_id=1, source_target_pairs={{0,10},{1,15},{2,12},{3,9},{4,14},{5,11},{6,8},{7,13},{8,2},{9,7},... | collective-permute-start | bytes 393224 | tf_op jit(solution)/shard_map/ppermute | solution.py:31
  97.6 10.9 %collective-permute-start.32 = (f32[256,768]{1,0:T(8,128)S(1)}, f32[256,768]{1,0:T(8,128)S(1)}, u32[]{:S(2)}, u32[]{:S(2)}) collective-permute-start(f32[256,768]{1,0:T(8,128)S(1)} %get-tuple-element.83), channel_id=1, source_target_pairs={{0,1},{1,0},{2,3},{3,2},{4,5},{5,4},{6,7},{7,6},{8,9},{9,8},{10,11... | collective-permute-start | bytes 2359304 | tf_op jit(solution)/shard_map/ppermute | solution.py:35
  110.8 13.1 %collective-permute-start.33 = (f32[64,512]{1,0:T(8,128)S(1)}, f32[64,512]{1,0:T(8,128)S(1)}, u32[]{:S(2)}, u32[]{:S(2)}) collective-permute-start(f32[64,512]{1,0:T(8,128)S(1)} %get-tuple-element.87), channel_id=1, source_target_pairs={{0,32},{16,48},{32,0},{48,16},{64,96},{80,112},{96,64},{112,80},{1... | collective-permute-start | bytes 393224 | tf_op jit(solution)/shard_map/ppermute | solution.py:23
  112.2 11.8 %collective-permute-start.34 = (f32[64,512]{1,0:T(8,128)S(1)}, f32[64,512]{1,0:T(8,128)S(1)}, u32[]{:S(2)}, u32[]{:S(2)}) collective-permute-start(f32[64,512]{1,0:T(8,128)S(1)} %get-tuple-element.88), channel_id=1, source_target_pairs={{0,16},{16,32},{32,48},{48,0},{64,80},{80,96},{96,112},{112,64},{1... | collective-permute-start | bytes 393224 | tf_op jit(solution)/shard_map/ppermute | solution.py:23
  114.0 10.0 %collective-permute-start.35 = (f32[64,512]{1,0:T(8,128)S(1)}, f32[64,512]{1,0:T(8,128)S(1)}, u32[]{:S(2)}, u32[]{:S(2)}) collective-permute-start(f32[64,512]{1,0:T(8,128)S(1)} %get-tuple-element.89), channel_id=1, source_target_pairs={{0,48},{16,0},{32,16},{48,32},{64,112},{80,64},{96,80},{112,96},{1... | collective-permute-start | bytes 393224 | tf_op jit(solution)/shard_map/ppermute | solution.py:23
  115.7 7.2 %collective-permute-start.22 = (f32[64,128]{1,0:T(8,128)S(1)}, f32[64,128]{1,0:T(8,128)S(1)}, u32[]{:S(2)}, u32[]{:S(2)}) collective-permute-start(f32[64,128]{1,0:T(8,128)S(1)} %get-tuple-element.78), channel_id=1, source_target_pairs={{0,16},{16,32},{32,48},{48,0},{64,80},{80,96},{96,112},{112,64},{1... | collective-permute-start | bytes 98312 | tf_op jit(solution)/shard_map/ppermute | solution.py:23
  (17 other events, 161.8 us)

commit v2 on v1

--- a/solution.py
+++ b/solution.py
@@ -275,18 +275,30 @@
     return call(kernel, [(pred.shape, F32)], where, [pred, *parts])[0]
 
 
-def solve(right_own, right_other, matrices, explicit_two, near_own, near_other, where):
+def begin_solve(right_own, matrix, explicit_two, near_own, near_other, where):
     half = right_own.shape[0]
+
+    def kernel(at, own_ref, high_ref, low_ref, explicit_ref, near_ref, far_ref, *outs):
+        mine = pl.ds(pl.multiple_of(at[0] * half, half), half)
+        matrix = (high_ref[:, mine], low_ref[:, mine])
+        outs[0][...] = narrow_product(matrix, split(own_ref[...]))
+        outs[1][...] = explicit_ref[:, lanes_from(at[1])] + (near_ref[...] + far_ref[...])
+
+    outs = [((2 * half, LANES), F32)] * 2
+    inputs = [right_own, *matrix, explicit_two, near_own, near_other]
+    return call(kernel, outs, where, inputs)
+
+
+def solve(begun, right_other, matrices, base, where):
+    half = right_other.shape[0]
     part = half // 4
 
-    def kernel(at, own_ref, other_ref, explicit_ref, near_ref, far_ref, *rest):
-        mats, (moved_ref, kept_ref), pieces = rest[:6], rest[6:8], rest[8:12]
-        right, first = rest[12:]
-        right[rows_from(at[0] * half, half), :] = own_ref[...]
-        right[rows_from((at[0] ^ 1) * half, half), :] = other_ref[...]
-        first[...] = narrow_product((mats[0][...], mats[1][...]), split(right[...]))
-        pred = explicit_ref[:, lanes_from(at[1])] + (near_ref[...] + far_ref[...])
-        pred = pred + narrow_product((mats[2][...], mats[3][...]), split(cubic_power(first[...])))
+    def kernel(at, begun_ref, other_ref, base_ref, *rest):
+        mats, (moved_ref, kept_ref), pieces, first = rest[:6], rest[6:8], rest[8:12], rest[12]
+        far = pl.ds(pl.multiple_of((at[0] ^ 1) * half, half), half)
+        matrix = (mats[0][:, far], mats[1][:, far])
+        first[...] = begun_ref[...] + narrow_product(matrix, split(other_ref[...]))
+        pred = base_ref[...] + narrow_product((mats[2][...], mats[3][...]), split(cubic_power(first[...])))
         both = jnp.concatenate([step_size * cubic_power(pred), pred], axis=1)
         solved = product((mats[4][...], mats[5][...]), split(both))
         moved_ref[...] = solved[:, :LANES]
@@ -295,8 +307,8 @@
             pieces[d][...] = first[rows_from((at[0] * 4 + ((at[1] + d) & 3)) * part, part), :]
 
     outs = [((half, LANES), F32)] * 2 + [((part, LANES), F32)] * 4
-    inputs = [right_own, right_other, explicit_two, near_own, near_other, *matrices]
-    return call(kernel, outs, where, inputs, (), [(2 * half, LANES)] * 2)
+    inputs = [begun, right_other, base, *matrices]
+    return call(kernel, outs, where, inputs, (), [(2 * half, LANES)])
 
 
 def add_pairs(blocks, where, after):
@@ -390,9 +402,9 @@
     near_other = move_hist(near, 1, 0)
 
     right = right_side(pred_one, parts, zx)
-    moved, kept, *pieces = solve(
-        right, move_hist(right, 1, 0), matrices, explicit_second, near, near_other, zx
-    )
+    right_other = move_hist(right, 1, 0)
+    begun, base = begin_solve(right, matrices[:2], explicit_second, near, near_other, zx)
+    moved, kept, *pieces = solve(begun, right_other, matrices, base, zx)
     begun, block = gathered(moved)
     pieces = over_x(pieces)
     blocks = finish_second(rows[2:], [block], zx, span_late, begun, kept)

time: 127 us -> 131 us (1.031)
  waiting for transfers between devices: 36.8 us -> 42 us
  starting transfers between devices: 56.7 us -> 54.9 us
    ppermute x18, waiting for transfers between devices: 21 us -> 26 us  [move_hist(): return lax.ppermute(value, 'hist', pairs)]
    ppermute x18, starting transfers between devices: 33.4 us -> 30 us  [move_hist(): return lax.ppermute(value, 'hist', pairs)]
    ppermute x4, starting transfers between devices: 9.81 us -> 11.8 us  [other_core(): return lax.ppermute(value, 'tcol', [(i, i ^ 1) for i in range(16)])]
    pallas_call x16 -> x17, Pallas kernels: 16.4 us -> 17 us  [call(): pl.pallas_call(body, in_specs=[SCALARS] + [WHOLE] * len(inputs) + [UNREAD...]
  transfers between devices with their start and end apart: 36 -> 36, of which waited for: 18 -> 17; matrix products, arithmetic and copies ran while one was open for 0% -> 0% of each run, Pallas kernels for 13% -> 14%
where the time goes in v2:
time: 131 us; the launch traced here: 129 us
  starting transfers between devices  54.9 us (42%)
  waiting for transfers between devices  42 us (32%)
  Pallas kernels  31.4 us (24%)
    ppermute x18, starting transfers between devices, move_hist(): return lax.ppermute(value, 'hist', pairs)  30 us
    ppermute x18, waiting for transfers between devices, move_hist(): return lax.ppermute(value, 'hist', pairs)  26 us
    pallas_call x17, Pallas kernels, call(): pl.pallas_call(body, in_specs=[SCALARS] + [WHOLE] * len(inputs) + [UNREAD...  17 us
    ppermute x14, waiting for transfers between devices, move_tcol(): return lax.ppermute(value, 'tcol', [(i, target(i)) for i in range(16)])  16 us
    ppermute x14, starting transfers between devices, move_tcol(): return lax.ppermute(value, 'tcol', [(i, target(i)) for i in range(16)])  13.2 us
    ppermute x4, starting transfers between devices, other_core(): return lax.ppermute(value, 'tcol', [(i, i ^ 1) for i in range(16)])  11.8 us
    pallas_call x2, Pallas kernels, collect(): pl.pallas_call(kernel, in_specs=[SCALARS, UNREAD, UNREAD] + [UNREAD] * n,...  11.5 us
    pallas_call x1, Pallas kernels, split_propagator(): pl.pallas_call(kernel, in_specs=[SCALARS, UNREAD, UNREAD], out_specs=[WHO...  2.87 us
  transfers between devices with their start and end apart: 36, of which 17 were waited for; matrix products, arithmetic and copies ran while one was open for 0% of the time, Pallas kernels for 14%

profile of v2, /device:TPU:1, one launch (start us, length us, event | category | flops | bytes accessed | tf_op | source)
XLA Modules:
  0.0 129.4 jit_solution(17358973802187627767)
XLA Ops:
  0.7 5.8 %collect.2 = (f32[2,256,128]{2,1,0:T(8,128)S(1)}, f32[2,256,128]{2,1,0:T(8,128)S(1)}, f32[2,256,128]{2,1,0:T(8,128)S(1)}, f32[2,256,128]{2,1,0:T(8,128)S(1)}) custom-call(s32[2]{0:T(128)S(1)} %pad_add_fusion.at, f32[2048,512]{1,0:T(8,128)} %hist_ref.3, f32[512,2048]{1,0:T(8,128)} %weight_ref.2), custom_call_target="tpu_custom_call" | custom-call | tf_op jit(solution)/shard_map/collect/pallas_call | solution.py:137
  6.5 3.6 %collective-permute-start = (f32[2,256,128]{2,1,0:T(8,128)S(1)}, f32[2,256,128]{2,1,0:T(8,128)S(1)}, u32[]{:S(2)}, u32[]{:S(2)}) collective-permute-start(f32[2,256,128]{2,1,0:T(8,128)S(1)} %get-tuple-element.49), channel_id=1, source_target_pairs={{0,32},{16,48},{32,0},{48,16},{64,96},{80,112},{96,64},{112,80},{1... | collective-permute-start | bytes 786440 | tf_op jit(solution)/shard_map/ppermute | solution.py:23
  10.5 2.4 %collective-permute-start.2 = (f32[2,256,128]{2,1,0:T(8,128)S(1)}, f32[2,256,128]{2,1,0:T(8,128)S(1)}, u32[]{:S(2)}, u32[]{:S(2)}) collective-permute-start(f32[2,256,128]{2,1,0:T(8,128)S(1)} %get-tuple-element.51), channel_id=1, source_target_pairs={{0,48},{16,0},{32,16},{48,32},{64,112},{80,64},{96,80},{112,96},{1... | collective-permute-start | bytes 786440 | tf_op jit(solution)/shard_map/ppermute | solution.py:23
  12.8 5.7 %collect.3.refs_4_.refs_0_._ = f32[512,512]{1,0:T(8,128)S(1)} custom-call(s32[2]{0:T(128)S(1)} %pad_add_fusion.at, f32[2048,512]{1,0:T(8,128)} %hist_ref.3, f32[512,2048]{1,0:T(8,128)} %weight_ref.3, f32[2,256,128]{2,1,0:T(8,128)S(1)} %get-tuple-element.48.rest_0_.refs_0_), custom_call_target="tpu_custom_call" | custom-call | tf_op jit(solution)/shard_map/collect/pallas_call | solution.py:137
  18.5 4.0 %collective-permute-done.1.refs_2_ = f32[2,256,128]{2,1,0:T(8,128)S(1)} collective-permute-done((f32[2,256,128]{2,1,0:T(8,128)S(1)}, f32[2,256,128]{2,1,0:T(8,128)S(1)}, u32[]{:S(2)}, u32[]{:S(2)}) %collective-permute-start.1) | collective-permute-done | bytes 262176 | tf_op jit(solution)/shard_map/ppermute | solution.py:23
  23.2 3.9 %collective-permute-start.3 = (f32[256,128]{1,0:T(8,128)S(1)}, f32[256,128]{1,0:T(8,128)S(1)}, u32[]{:S(2)}, u32[]{:S(2)}) collective-permute-start(f32[256,128]{1,0:T(8,128)S(1)} %get-tuple-element.53.refs_1_), channel_id=1, source_target_pairs={{0,64},{16,80},{32,96},{48,112},{64,0},{80,16},{96,32},{112,48},{1... | collective-permute-start | bytes 393224 | tf_op jit(solution)/shard_map/ppermute | solution.py:23
  27.8 2.6 %collective-permute-done.3.refs_2_ = f32[256,128]{1,0:T(8,128)S(1)} collective-permute-done((f32[256,128]{1,0:T(8,128)S(1)}, f32[256,128]{1,0:T(8,128)S(1)}, u32[]{:S(2)}, u32[]{:S(2)}) %collective-permute-start.3) | collective-permute-done | bytes 131104 | tf_op jit(solution)/shard_map/ppermute | solution.py:23
  36.9 2.9 %split_propagator.1 = (bf16[1024,512]{1,0:T(8,128)(2,1)S(1)}, bf16[1024,512]{1,0:T(8,128)(2,1)S(1)}, bf16[1024,512]{1,0:T(8,128)(2,1)S(1)}, bf16[1024,512]{1,0:T(8,128)(2,1)S(1)}) custom-call(s32[17]{0:T(128)S(1)} %stack.80.at, f32[16,4,128,512]{3,2,1,0:T(8,128)} %bitcast.19, f32[512,512]{1,0:T(8,128)S(1)} %collect.3.refs_4_.refs_0_._), custom_call_target="tpu_custom_call" | custom-call | tf_op jit(solution)/shard_map/split_propagator/pallas_call | solution.py:175
  40.3 2.3 %collective-permute-done.4.refs_3_ = f32[256,128]{1,0:T(8,128)S(1)} collective-permute-done((f32[256,128]{1,0:T(8,128)S(1)}, f32[256,128]{1,0:T(8,128)S(1)}, u32[]{:S(2)}, u32[]{:S(2)}) %collective-permute-start.4) | collective-permute-done | bytes 131104 | tf_op jit(solution)/shard_map/ppermute | solution.py:31
  44.0 3.1 %collective-permute-start.12 = (f32[256,768]{1,0:T(8,128)S(1)}, f32[256,768]{1,0:T(8,128)S(1)}, u32[]{:S(2)}, u32[]{:S(2)}) collective-permute-start(f32[256,768]{1,0:T(8,128)S(1)} %get-tuple-element.63), channel_id=1, source_target_pairs={{0,1},{1,0},{2,3},{3,2},{4,5},{5,4},{6,7},{7,6},{8,9},{9,8},{10,11... | collective-permute-start | bytes 2359304 | tf_op jit(solution)/shard_map/ppermute | solution.py:35
  48.0 2.9 %collective-permute-done.7.refs_3_ = f32[256,128]{1,0:T(8,128)S(1)} collective-permute-done((f32[256,128]{1,0:T(8,128)S(1)}, f32[256,128]{1,0:T(8,128)S(1)}, u32[]{:S(2)}, u32[]{:S(2)}) %collective-permute-start.7) | collective-permute-done | bytes 131104 | tf_op jit(solution)/shard_map/ppermute | solution.py:31
  53.5 2.2 %collective-permute-start.11 = (f32[256,256]{1,0:T(8,128)S(1)}, f32[256,256]{1,0:T(8,128)S(1)}, u32[]{:S(2)}, u32[]{:S(2)}) collective-permute-start(f32[256,256]{1,0:T(8,128)S(1)} %get-tuple-element.62), channel_id=1, source_target_pairs={{0,1},{1,0},{2,3},{3,2},{4,5},{5,4},{6,7},{7,6},{8,9},{9,8},{10,11... | collective-permute-start | bytes 786440 | tf_op jit(solution)/shard_map/ppermute | solution.py:35
  65.1 6.5 %collective-permute-done.17.refs_2_ = f32[512,128]{1,0:T(8,128)S(1)} collective-permute-done((f32[512,128]{1,0:T(8,128)S(1)}, f32[512,128]{1,0:T(8,128)S(1)}, u32[]{:S(2)}, u32[]{:S(2)}) %collective-permute-start.17) | collective-permute-done | bytes 262176 | tf_op jit(solution)/shard_map/ppermute | solution.py:23
  72.2 3.4 %collective-permute-start.19 = (f32[512,128]{1,0:T(8,128)S(1)}, f32[512,128]{1,0:T(8,128)S(1)}, u32[]{:S(2)}, u32[]{:S(2)}) collective-permute-start(f32[512,128]{1,0:T(8,128)S(1)} %shard_map.113.refs_4_), channel_id=1, source_target_pairs={{0,64},{16,80},{32,96},{48,112},{64,0},{80,16},{96,32},{112,48},{1... | collective-permute-start | bytes 786440 | tf_op jit(solution)/shard_map/ppermute | solution.py:23
  78.2 2.6 %collective-permute-done.14.refs_3_ = f32[256,128]{1,0:T(8,128)S(1)} collective-permute-done((f32[256,128]{1,0:T(8,128)S(1)}, f32[256,128]{1,0:T(8,128)S(1)}, u32[]{:S(2)}, u32[]{:S(2)}) %collective-permute-start.14) | collective-permute-done | bytes 131104 | tf_op jit(solution)/shard_map/ppermute | solution.py:23
  83.7 3.2 %collective-permute-done.20.refs_1_ = f32[256,128]{1,0:T(8,128)S(1)} collective-permute-done((f32[256,128]{1,0:T(8,128)S(1)}, f32[256,128]{1,0:T(8,128)S(1)}, u32[]{:S(2)}, u32[]{:S(2)}) %collective-permute-start.20) | collective-permute-done | bytes 131104 | tf_op jit(solution)/shard_map/ppermute | solution.py:23
  89.2 3.4 %collective-permute-start.26 = (f32[256,128]{1,0:T(8,128)S(1)}, f32[256,128]{1,0:T(8,128)S(1)}, u32[]{:S(2)}, u32[]{:S(2)}) collective-permute-start(f32[256,128]{1,0:T(8,128)S(1)} %get-tuple-element.84.refs_2_), channel_id=1, source_target_pairs={{0,10},{1,15},{2,12},{3,9},{4,14},{5,11},{6,8},{7,13},{8,2},{9,7},... | collective-permute-start | bytes 393224 | tf_op jit(solution)/shard_map/ppermute | solution.py:31
  94.0 2.6 %collective-permute-done.28.refs_5_ = f32[256,128]{1,0:T(8,128)S(1)} collective-permute-done((f32[256,128]{1,0:T(8,128)S(1)}, f32[256,128]{1,0:T(8,128)S(1)}, u32[]{:S(2)}, u32[]{:S(2)}) %collective-permute-start.28) | collective-permute-done | bytes 131104 | tf_op jit(solution)/shard_map/ppermute | solution.py:31
  99.5 4.2 %collective-permute-start.32 = (f32[256,768]{1,0:T(8,128)S(1)}, f32[256,768]{1,0:T(8,128)S(1)}, u32[]{:S(2)}, u32[]{:S(2)}) collective-permute-start(f32[256,768]{1,0:T(8,128)S(1)} %get-tuple-element.87), channel_id=1, source_target_pairs={{0,1},{1,0},{2,3},{3,2},{4,5},{5,4},{6,7},{7,6},{8,9},{9,8},{10,11... | collective-permute-start | bytes 2359304 | tf_op jit(solution)/shard_map/ppermute | solution.py:35
  105.0 2.6 %collective-permute-done.27.refs_3_ = f32[256,128]{1,0:T(8,128)S(1)} collective-permute-done((f32[256,128]{1,0:T(8,128)S(1)}, f32[256,128]{1,0:T(8,128)S(1)}, u32[]{:S(2)}, u32[]{:S(2)}) %collective-permute-start.27) | collective-permute-done | bytes 131104 | tf_op jit(solution)/shard_map/ppermute | solution.py:31
  110.2 2.2 %collective-permute-start.31 = (f32[256,256]{1,0:T(8,128)S(1)}, f32[256,256]{1,0:T(8,128)S(1)}, u32[]{:S(2)}, u32[]{:S(2)}) collective-permute-start(f32[256,256]{1,0:T(8,128)S(1)} %get-tuple-element.86), channel_id=1, source_target_pairs={{0,1},{1,0},{2,3},{3,2},{4,5},{5,4},{6,7},{7,6},{8,9},{9,8},{10,11... | collective-permute-start | bytes 786440 | tf_op jit(solution)/shard_map/ppermute | solution.py:35
  114.7 2.5 %collective-permute-start.33 = (f32[64,512]{1,0:T(8,128)S(1)}, f32[64,512]{1,0:T(8,128)S(1)}, u32[]{:S(2)}, u32[]{:S(2)}) collective-permute-start(f32[64,512]{1,0:T(8,128)S(1)} %get-tuple-element.91), channel_id=1, source_target_pairs={{0,32},{16,48},{32,0},{48,16},{64,96},{80,112},{96,64},{112,80},{1... | collective-permute-start | bytes 393224 | tf_op jit(solution)/shard_map/ppermute | solution.py:23
  120.4 4.0 %collective-permute-done.21.refs_1_ = f32[64,128]{1,0:T(8,128)S(1)} collective-permute-done((f32[64,128]{1,0:T(8,128)S(1)}, f32[64,128]{1,0:T(8,128)S(1)}, u32[]{:S(2)}, u32[]{:S(2)}) %collective-permute-start.21) | collective-permute-done | bytes 32800 | tf_op jit(solution)/shard_map/ppermute | solution.py:23
  124.5 2.6 %collective-permute-start.23 = (f32[64,128]{1,0:T(8,128)S(1)}, f32[64,128]{1,0:T(8,128)S(1)}, u32[]{:S(2)}, u32[]{:S(2)}) collective-permute-start(f32[64,128]{1,0:T(8,128)S(1)} %get-tuple-element.83), channel_id=1, source_target_pairs={{0,48},{16,0},{32,16},{48,32},{64,112},{80,64},{96,80},{112,96},{1... | collective-permute-start | bytes 98312 | tf_op jit(solution)/shard_map/ppermute | solution.py:23
  (80 shorter events, 47.2 us)
Async XLA Ops:
  6.5 12.0 %collective-permute-start = (f32[2,256,128]{2,1,0:T(8,128)S(1)}, f32[2,256,128]{2,1,0:T(8,128)S(1)}, u32[]{:S(2)}, u32[]{:S(2)}) collective-permute-start(f32[2,256,128]{2,1,0:T(8,128)S(1)} %get-tuple-element.49), channel_id=1, source_target_pairs={{0,32},{16,48},{32,0},{48,16},{64,96},{80,112},{96,64},{112,80},{1... | collective-permute-start | bytes 786440 | tf_op jit(solution)/shard_map/ppermute | solution.py:23
  10.2 12.4 %collective-permute-start.1 = (f32[2,256,128]{2,1,0:T(8,128)S(1)}, f32[2,256,128]{2,1,0:T(8,128)S(1)}, u32[]{:S(2)}, u32[]{:S(2)}) collective-permute-start(f32[2,256,128]{2,1,0:T(8,128)S(1)} %get-tuple-element.50), channel_id=1, source_target_pairs={{0,16},{16,32},{32,48},{48,0},{64,80},{80,96},{96,112},{112,64},{1... | collective-permute-start | bytes 786440 | tf_op jit(solution)/shard_map/ppermute | solution.py:23
  10.5 12.1 %collective-permute-start.2 = (f32[2,256,128]{2,1,0:T(8,128)S(1)}, f32[2,256,128]{2,1,0:T(8,128)S(1)}, u32[]{:S(2)}, u32[]{:S(2)}) collective-permute-start(f32[2,256,128]{2,1,0:T(8,128)S(1)} %get-tuple-element.51), channel_id=1, source_target_pairs={{0,48},{16,0},{32,16},{48,32},{64,112},{80,64},{96,80},{112,96},{1... | collective-permute-start | bytes 786440 | tf_op jit(solution)/shard_map/ppermute | solution.py:23
  23.2 7.2 %collective-permute-start.3 = (f32[256,128]{1,0:T(8,128)S(1)}, f32[256,128]{1,0:T(8,128)S(1)}, u32[]{:S(2)}, u32[]{:S(2)}) collective-permute-start(f32[256,128]{1,0:T(8,128)S(1)} %get-tuple-element.53.refs_1_), channel_id=1, source_target_pairs={{0,64},{16,80},{32,96},{48,112},{64,0},{80,16},{96,32},{112,48},{1... | collective-permute-start | bytes 393224 | tf_op jit(solution)/shard_map/ppermute | solution.py:23
  30.9 8.8 %collective-permute-start.10 = (f32[256,128]{1,0:T(8,128)S(1)}, f32[256,128]{1,0:T(8,128)S(1)}, u32[]{:S(2)}, u32[]{:S(2)}) collective-permute-start(f32[256,128]{1,0:T(8,128)S(1)} %get-tuple-element.60.refs_2_), channel_id=1, source_target_pairs={{0,8},{1,9},{2,10},{3,11},{4,12},{5,13},{6,14},{7,15},{8,0},{9,1},... | collective-permute-start | bytes 393224 | tf_op jit(solution)/shard_map/ppermute | solution.py:31
  31.7 8.0 %collective-permute-start.9 = (f32[256,128]{1,0:T(8,128)S(1)}, f32[256,128]{1,0:T(8,128)S(1)}, u32[]{:S(2)}, u32[]{:S(2)}) collective-permute-start(f32[256,128]{1,0:T(8,128)S(1)} %get-tuple-element.60.refs_2_), channel_id=1, source_target_pairs={{0,6},{1,3},{2,0},{3,5},{4,2},{5,7},{6,4},{7,1},{8,14},{9,11},{10,... | collective-permute-start | bytes 393224 | tf_op jit(solution)/shard_map/ppermute | solution.py:31
  33.0 6.8 %collective-permute-start.8 = (f32[256,128]{1,0:T(8,128)S(1)}, f32[256,128]{1,0:T(8,128)S(1)}, u32[]{:S(2)}, u32[]{:S(2)}) collective-permute-start(f32[256,128]{1,0:T(8,128)S(1)} %get-tuple-element.60.refs_2_), channel_id=1, source_target_pairs={{0,14},{1,11},{2,8},{3,13},{4,10},{5,15},{6,12},{7,9},{8,6},{9,3},... | collective-permute-start | bytes 393224 | tf_op jit(solution)/shard_map/ppermute | solution.py:31
  34.7 5.6 %collective-permute-start.6 = (f32[256,128]{1,0:T(8,128)S(1)}, f32[256,128]{1,0:T(8,128)S(1)}, u32[]{:S(2)}, u32[]{:S(2)}) collective-permute-start(f32[256,128]{1,0:T(8,128)S(1)} %get-tuple-element.60.refs_2_), channel_id=1, source_target_pairs={{0,10},{1,15},{2,12},{3,9},{4,14},{5,11},{6,8},{7,13},{8,2},{9,7},... | collective-permute-start | bytes 393224 | tf_op jit(solution)/shard_map/ppermute | solution.py:31
  36.6 6.1 %collective-permute-start.4 = (f32[256,128]{1,0:T(8,128)S(1)}, f32[256,128]{1,0:T(8,128)S(1)}, u32[]{:S(2)}, u32[]{:S(2)}) collective-permute-start(f32[256,128]{1,0:T(8,128)S(1)} %get-tuple-element.60.refs_2_), channel_id=1, source_target_pairs={{0,2},{1,7},{2,4},{3,1},{4,6},{5,3},{6,0},{7,5},{8,10},{9,15},{10,... | collective-permute-start | bytes 393224 | tf_op jit(solution)/shard_map/ppermute | solution.py:31
  44.0 15.9 %collective-permute-start.12 = (f32[256,768]{1,0:T(8,128)S(1)}, f32[256,768]{1,0:T(8,128)S(1)}, u32[]{:S(2)}, u32[]{:S(2)}) collective-permute-start(f32[256,768]{1,0:T(8,128)S(1)} %get-tuple-element.63), channel_id=1, source_target_pairs={{0,1},{1,0},{2,3},{3,2},{4,5},{5,4},{6,7},{7,6},{8,9},{9,8},{10,11... | collective-permute-start | bytes 2359304 | tf_op jit(solution)/shard_map/ppermute | solution.py:35
  53.5 7.7 %collective-permute-start.11 = (f32[256,256]{1,0:T(8,128)S(1)}, f32[256,256]{1,0:T(8,128)S(1)}, u32[]{:S(2)}, u32[]{:S(2)}) collective-permute-start(f32[256,256]{1,0:T(8,128)S(1)} %get-tuple-element.62), channel_id=1, source_target_pairs={{0,1},{1,0},{2,3},{3,2},{4,5},{5,4},{6,7},{7,6},{8,9},{9,8},{10,11... | collective-permute-start | bytes 786440 | tf_op jit(solution)/shard_map/ppermute | solution.py:35
  55.8 9.3 %collective-permute-start.16 = (f32[512,128]{1,0:T(8,128)S(1)}, f32[512,128]{1,0:T(8,128)S(1)}, u32[]{:S(2)}, u32[]{:S(2)}) collective-permute-start(f32[512,128]{1,0:T(8,128)S(1)} %get-tuple-element.71), channel_id=1, source_target_pairs={{0,32},{16,48},{32,0},{48,16},{64,96},{80,112},{96,64},{112,80},{1... | collective-permute-start | bytes 786440 | tf_op jit(solution)/shard_map/ppermute | solution.py:23
  57.2 14.3 %collective-permute-start.17 = (f32[512,128]{1,0:T(8,128)S(1)}, f32[512,128]{1,0:T(8,128)S(1)}, u32[]{:S(2)}, u32[]{:S(2)}) collective-permute-start(f32[512,128]{1,0:T(8,128)S(1)} %get-tuple-element.72), channel_id=1, source_target_pairs={{0,16},{16,32},{32,48},{48,0},{64,80},{80,96},{96,112},{112,64},{1... | collective-permute-start | bytes 786440 | tf_op jit(solution)/shard_map/ppermute | solution.py:23
  58.8 12.7 %collective-permute-start.18 = (f32[512,128]{1,0:T(8,128)S(1)}, f32[512,128]{1,0:T(8,128)S(1)}, u32[]{:S(2)}, u32[]{:S(2)}) collective-permute-start(f32[512,128]{1,0:T(8,128)S(1)} %get-tuple-element.73), channel_id=1, source_target_pairs={{0,48},{16,0},{32,16},{48,32},{64,112},{80,64},{96,80},{112,96},{1... | collective-permute-start | bytes 786440 | tf_op jit(solution)/shard_map/ppermute | solution.py:23
  62.2 16.0 %collective-permute-start.13 = (f32[256,128]{1,0:T(8,128)S(1)}, f32[256,128]{1,0:T(8,128)S(1)}, u32[]{:S(2)}, u32[]{:S(2)}) collective-permute-start(f32[256,128]{1,0:T(8,128)S(1)} %get-tuple-element.66), channel_id=1, source_target_pairs={{0,32},{16,48},{32,0},{48,16},{64,96},{80,112},{96,64},{112,80},{1... | collective-permute-start | bytes 393224 | tf_op jit(solution)/shard_map/ppermute | solution.py:23
  72.2 10.7 %collective-permute-start.19 = (f32[512,128]{1,0:T(8,128)S(1)}, f32[512,128]{1,0:T(8,128)S(1)}, u32[]{:S(2)}, u32[]{:S(2)}) collective-permute-start(f32[512,128]{1,0:T(8,128)S(1)} %shard_map.113.refs_4_), channel_id=1, source_target_pairs={{0,64},{16,80},{32,96},{48,112},{64,0},{80,16},{96,32},{112,48},{1... | collective-permute-start | bytes 786440 | tf_op jit(solution)/shard_map/ppermute | solution.py:23
  88.9 7.6 %collective-permute-start.28 = (f32[256,128]{1,0:T(8,128)S(1)}, f32[256,128]{1,0:T(8,128)S(1)}, u32[]{:S(2)}, u32[]{:S(2)}) collective-permute-start(f32[256,128]{1,0:T(8,128)S(1)} %get-tuple-element.84.refs_2_), channel_id=1, source_target_pairs={{0,14},{1,11},{2,8},{3,13},{4,10},{5,15},{6,12},{7,9},{8,6},{9,3},... | collective-permute-start | bytes 393224 | tf_op jit(solution)/shard_map/ppermute | solution.py:31
  89.2 7.3 %collective-permute-start.26 = (f32[256,128]{1,0:T(8,128)S(1)}, f32[256,128]{1,0:T(8,128)S(1)}, u32[]{:S(2)}, u32[]{:S(2)}) collective-permute-start(f32[256,128]{1,0:T(8,128)S(1)} %get-tuple-element.84.refs_2_), channel_id=1, source_target_pairs={{0,10},{1,15},{2,12},{3,9},{4,14},{5,11},{6,8},{7,13},{8,2},{9,7},... | collective-permute-start | bytes 393224 | tf_op jit(solution)/shard_map/ppermute | solution.py:31
  92.7 5.5 %collective-permute-start.24 = (f32[256,128]{1,0:T(8,128)S(1)}, f32[256,128]{1,0:T(8,128)S(1)}, u32[]{:S(2)}, u32[]{:S(2)}) collective-permute-start(f32[256,128]{1,0:T(8,128)S(1)} %get-tuple-element.84.refs_2_), channel_id=1, source_target_pairs={{0,2},{1,7},{2,4},{3,1},{4,6},{5,3},{6,0},{7,5},{8,10},{9,15},{10,... | collective-permute-start | bytes 393224 | tf_op jit(solution)/shard_map/ppermute | solution.py:31
  99.5 12.9 %collective-permute-start.32 = (f32[256,768]{1,0:T(8,128)S(1)}, f32[256,768]{1,0:T(8,128)S(1)}, u32[]{:S(2)}, u32[]{:S(2)}) collective-permute-start(f32[256,768]{1,0:T(8,128)S(1)} %get-tuple-element.87), channel_id=1, source_target_pairs={{0,1},{1,0},{2,3},{3,2},{4,5},{5,4},{6,7},{7,6},{8,9},{9,8},{10,11... | collective-permute-start | bytes 2359304 | tf_op jit(solution)/shard_map/ppermute | solution.py:35
  114.7 13.4 %collective-permute-start.33 = (f32[64,512]{1,0:T(8,128)S(1)}, f32[64,512]{1,0:T(8,128)S(1)}, u32[]{:S(2)}, u32[]{:S(2)}) collective-permute-start(f32[64,512]{1,0:T(8,128)S(1)} %get-tuple-element.91), channel_id=1, source_target_pairs={{0,32},{16,48},{32,0},{48,16},{64,96},{80,112},{96,64},{112,80},{1... | collective-permute-start | bytes 393224 | tf_op jit(solution)/shard_map/ppermute | solution.py:23
  117.2 10.9 %collective-permute-start.34 = (f32[64,512]{1,0:T(8,128)S(1)}, f32[64,512]{1,0:T(8,128)S(1)}, u32[]{:S(2)}, u32[]{:S(2)}) collective-permute-start(f32[64,512]{1,0:T(8,128)S(1)} %get-tuple-element.92), channel_id=1, source_target_pairs={{0,16},{16,32},{32,48},{48,0},{64,80},{80,96},{96,112},{112,64},{1... | collective-permute-start | bytes 393224 | tf_op jit(solution)/shard_map/ppermute | solution.py:23
  118.1 10.0 %collective-permute-start.35 = (f32[64,512]{1,0:T(8,128)S(1)}, f32[64,512]{1,0:T(8,128)S(1)}, u32[]{:S(2)}, u32[]{:S(2)}) collective-permute-start(f32[64,512]{1,0:T(8,128)S(1)} %get-tuple-element.93), channel_id=1, source_target_pairs={{0,48},{16,0},{32,16},{48,32},{64,112},{80,64},{96,80},{112,96},{1... | collective-permute-start | bytes 393224 | tf_op jit(solution)/shard_map/ppermute | solution.py:23
  119.9 7.2 %collective-permute-start.22 = (f32[64,128]{1,0:T(8,128)S(1)}, f32[64,128]{1,0:T(8,128)S(1)}, u32[]{:S(2)}, u32[]{:S(2)}) collective-permute-start(f32[64,128]{1,0:T(8,128)S(1)} %get-tuple-element.82), channel_id=1, source_target_pairs={{0,16},{16,32},{32,48},{48,0},{64,80},{80,96},{96,112},{112,64},{1... | collective-permute-start | bytes 98312 | tf_op jit(solution)/shard_map/ppermute | solution.py:23
  (17 other events, 158.7 us)
